TPU v7x, 32 devices: a whole 2x2x4 slice. The times are simulated.
32 devices in a mesh: row: 16 (over z, y, core), rep: 2 (over x).
Axes of the slice: x: 2, y: 2, z: 4, core: 2. Of those that a mesh axis runs over, the one named last changes fastest.
Arguments:
- features: bfloat16 [8192, 128], P('row'), may hold values from -6 to 6
- input_weight: bfloat16 [128, 512], replicated, may hold values from -5 to 5
- output_weight: bfloat16 [512, 512], replicated, may hold values from -0.25 to 0.25
- cotangent: bfloat16 [8192, 512], P(('row', 'rep')), may hold values from -0.25 to 0.25
- adjacency_tiles: bfloat16 [64, 8, 128, 128], P('row', 'rep'), may hold values from 0.0009994507 to 1
- block_columns: int32 [64, 8], P('row', 'rep'), may hold values from 0 to 63, as said below
- graph_sizes: int32 [16], replicated, may hold values from 1 to 2048, 8192 in all
Outputs:
- scores: bfloat16 [8192, 512], P(('row', 'rep'))
- grad_input: float32 [128, 512], replicated
- grad_output: float32 [512, 512], replicated
Inputs may be any that keep to these rules, and one draw needn't show every extreme that they name: `block_columns`: each row block b lists 8 distinct column blocks, its own first, every one within 12 blocks of b along the closed loop of 64 blocks (indices taken mod 64); row block 0 lists the blocks at both ends of that reach. `graph_sizes`: the sizes sum to 8192.
All inputs are finite; a program needn't handle non-finite values.
Results may differ from a plain program's by a relative error of at most 0.0045.
The roundings to bfloat16 on the way count: a program that leaves them out, or rounds other values in their place, can miss the bound.
Values may be sent and summed in bfloat16 or wider, within the bound.
A program may use at most 64 MiB of HBM per device.

v0:
```python
import jax
import jax.numpy as jnp
from jax import lax
from jax.sharding import PartitionSpec as P

HOPS = 3


def passed_along(shard, axis, by):
    peers = lax.axis_size(axis)
    return lax.ppermute(shard, axis, [(i, (i + by) % peers) for i in range(peers)])


def graph_of(nodes, ends):
    return jnp.sum((nodes[..., None] >= ends).astype(jnp.int32), axis=-1)


def move_input(value, offset):
    return passed_along(value, "row", offset)


def move_hidden(value, offset):
    return passed_along(value, "row", offset)


def move_terms(value, offset):
    return passed_along(value.astype(jnp.bfloat16), "row", offset).astype(value.dtype)


def rep_reduce(parts):
    return lax.psum_scatter(parts, "rep", scatter_dimension=0, tiled=True)


def share_rows(value):
    return lax.all_gather(value, "rep", axis=0, tiled=True)


def band_collect(local, mover):
    held_by = {0: local}
    for sign in (1, -1):
        held = local
        for step in range(1, HOPS + 1):
            held = mover(held, -sign)
            held_by[sign * step] = held
    return held_by


def band_stack(held_by, blocks, tile):
    return jnp.concatenate(
        [held_by[shift].reshape(blocks, tile, -1) for shift in range(-HOPS, HOPS + 1)], axis=0
    )


def band_gather(held_by, placing, blocks, tile):
    gathered = jnp.einsum(
        "bkm,mjf->bkjf",
        placing,
        band_stack(held_by, blocks, tile),
        preferred_element_type=jnp.float32,
    )
    return gathered.astype(jnp.bfloat16)


def body(
    features, input_weight, output_weight, cotangent, adjacency_tiles, block_columns, graph_sizes
):
    row_index = lax.axis_index("row")
    row_count = lax.axis_size("row")
    rep_index = lax.axis_index("rep")
    rep_count = lax.axis_size("rep")
    blocks = adjacency_tiles.shape[0]
    tile = adjacency_tiles.shape[2]
    local_rows = blocks * tile
    quarter = local_rows // rep_count
    ends = jnp.cumsum(graph_sizes)
    within = jnp.arange(tile, dtype=jnp.int32)
    row_nodes = (row_index * blocks + jnp.arange(blocks, dtype=jnp.int32))[:, None] * tile + within
    col_nodes = block_columns[..., None] * tile + within
    same = graph_of(row_nodes, ends)[:, None, :, None] == graph_of(col_nodes, ends)[:, :, None, :]
    masked = jnp.where(same, adjacency_tiles, jnp.zeros_like(adjacency_tiles))
    holder = block_columns // blocks
    distance = (holder - row_index + HOPS) % row_count - HOPS
    position = block_columns - holder * blocks
    band_slots = jnp.arange((2 * HOPS + 1) * blocks, dtype=jnp.int32)
    tile_slot = (distance + HOPS) * blocks + position
    placing_all = (tile_slot[..., None] == band_slots).astype(jnp.bfloat16)

    def aggregate(gathered):
        return jnp.einsum(
            "bkij,bkjf->bif", masked, gathered, preferred_element_type=jnp.float32
        ).reshape(local_rows, -1)

    own_feats = lax.dynamic_slice_in_dim(features, rep_index * quarter, quarter, 0).astype(
        jnp.float32
    )
    feats_by = band_collect(features, move_input)
    row_sums = jnp.sum(masked.astype(jnp.float32), axis=(1, 3)).reshape(local_rows)
    gathered_in = band_gather(feats_by, placing_all, blocks, tile)
    summed_in, summed_rows = rep_reduce((aggregate(gathered_in), row_sums))
    degree = 1.0 + summed_rows
    first = ((summed_in + own_feats) / degree[:, None]).astype(jnp.bfloat16)
    preact = jnp.dot(first, input_weight, preferred_element_type=jnp.float32)
    hidden_part = jnp.maximum(preact, 0.0).astype(jnp.bfloat16)
    hidden_full = share_rows(hidden_part)
    hidden_by = band_collect(hidden_full, move_hidden)
    gathered_hid = band_gather(hidden_by, placing_all, blocks, tile)
    (summed_hid,) = rep_reduce((aggregate(gathered_hid),))
    second = ((summed_hid + hidden_part.astype(jnp.float32)) / degree[:, None]).astype(jnp.bfloat16)
    scores = jnp.dot(second, output_weight, preferred_element_type=jnp.float32).astype(jnp.bfloat16)
    grad_output = lax.dot_general(
        second, cotangent, (((0,), (0,)), ((), ())), preferred_element_type=jnp.float32
    )
    pulled = lax.dot_general(
        cotangent, output_weight, (((1,), (1,)), ((), ())), preferred_element_type=jnp.float32
    )
    scaled_part = (pulled / degree[:, None]).astype(jnp.bfloat16)
    scaled_full = share_rows(scaled_part)
    scaled_blocks = scaled_full.reshape(blocks, tile, -1)
    product = jnp.einsum(
        "bkij,bif->bkjf", masked, scaled_blocks, preferred_element_type=jnp.float32
    )
    shares = jnp.einsum("bkm,bkjf->mjf", placing_all.astype(jnp.float32), product)
    shares = shares.reshape(2 * HOPS + 1, blocks, tile, -1)

    def portion(shift):
        return shares[shift + HOPS]

    total = portion(0)
    for sign in (1, -1):
        carried = portion(sign * HOPS)
        for step in range(HOPS - 1, 0, -1):
            carried = move_terms(carried, sign) + portion(sign * step)
        total = total + move_terms(carried, sign)
    (transposed,) = rep_reduce((total.reshape(local_rows, -1),))
    back = transposed + scaled_part.astype(jnp.float32)
    delta = jnp.where(preact > 0.0, back, 0.0).astype(jnp.bfloat16)
    grad_input = lax.dot_general(
        first, delta, (((0,), (0,)), ((), ())), preferred_element_type=jnp.float32
    )
    grad_input, grad_output = lax.psum((grad_input, grad_output), ("row", "rep"))
    return (scores, grad_input, grad_output)


def solution(mesh):
    placed = (
        P("row", None),
        P(),
        P(),
        P(("row", "rep"), None),
        P("row", "rep", None, None),
        P("row", "rep"),
        P(),
    )
    return jax.shard_map(
        body,
        mesh=mesh,
        in_specs=placed,
        out_specs=(P(("row", "rep"), None), P(), P()),
        check_vma=False,
    )
```

profile of v0, /device:TPU:0, one launch (start us, length us, event | category | flops | bytes accessed | tf_op | source)
XLA Modules:
  0.0 339.2 jit_solution(13292127404870751406)
XLA Ops:
  10.6 5.8 %all-reduce = f32[512]{0:T(512)S(1)} all-reduce(f32[512]{0:T(512)S(1)} %bitcast.80), channel_id=3, replica_groups=mesh['row'=16,'rep'=2] {'rep'}, use_global_device_ids=true, to_apply=%region_5.6.clone | all-reduce | flops 512 | bytes 4096
  19.7 7.9 %all_gather.7 = bf16[512,512]{1,0:T(8,128)(2,1)S(1)} all-gather(bf16[256,512]{1,0:T(8,128)(2,1)S(1)} %fusion.12), channel_id=1, replica_groups=mesh['row'=16,'rep'=2] {'rep'}, dimensions={0}, use_global_device_ids=true | all-gather | bytes 786432 | tf_op jit(solution)/shard_map/all_gather | solution.py:35
  28.5 6.3 %fusion.42 = (bf16[28,128,512]{2,0,1:T(8,128)(2,1)S(1)}, f32[28,128,512]{2,0,1:T(8,128)}) fusion(bf16[4,4,128,512]{3,2,1,0:T(8,128)(2,1)S(1)} %fusion.23, s32[4,4]{1,0:T(4,128)S(1)} %get-tuple-element.12), kind=kOutput, calls=%fused_computation.65 | convolution fusion | flops 60555712 | bytes 13107264 | tf_op jit(solution)/shard_map/bkm,bkjf->mjf/dot_general | solution.py:122
  35.2 4.4 %collective-permute-start.15 = (bf16[4,128,512]{2,0,1:T(4,128)(2,1)S(1)}, bf16[4,128,512]{2,0,1:T(4,128)(2,1)}, u32[]{:S(2)}, u32[]{:S(2)}) collective-permute-start(bf16[4,128,512]{2,0,1:T(4,128)(2,1)S(1)} %get-tuple-element.10), channel_id=1, source_target_pairs={{0,30},{2,0},{4,2},{6,4},{8,6},{10,8},{12,10},{14,12},{16,14},{18,... | collective-permute-start | bytes 1572872 | tf_op jit(solution)/shard_map/ppermute | solution.py:11
  39.6 4.4 %collective-permute-start.3 = (bf16[512,128]{1,0:T(8,128)(2,1)S(1)}, bf16[512,128]{1,0:T(8,128)(2,1)S(1)}, u32[]{:S(2)}, u32[]{:S(2)}) collective-permute-start(bf16[512,128]{1,0:T(8,128)(2,1)S(1)} %copy-done.5), channel_id=1, source_target_pairs={{0,30},{2,0},{4,2},{6,4},{8,6},{10,8},{12,10},{14,12},{16,14},{18,... | collective-permute-start | bytes 393224 | tf_op jit(solution)/shard_map/ppermute | solution.py:11
  44.0 3.9 %collective-permute-done = bf16[512,128]{1,0:T(8,128)(2,1)S(1)} collective-permute-done((bf16[512,128]{1,0:T(8,128)(2,1)S(1)}, bf16[512,128]{1,0:T(8,128)(2,1)S(1)}, u32[]{:S(2)}, u32[]{:S(2)}) %collective-permute-start) | collective-permute-done | bytes 131104 | tf_op jit(solution)/shard_map/ppermute | solution.py:11
  48.0 3.6 %collective-permute-start.1 = (bf16[512,128]{1,0:T(8,128)(2,1)S(1)}, bf16[512,128]{1,0:T(8,128)(2,1)S(1)}, u32[]{:S(2)}, u32[]{:S(2)}) collective-permute-start(bf16[512,128]{1,0:T(8,128)(2,1)S(1)} %collective-permute-done), channel_id=1, source_target_pairs={{0,2},{2,4},{4,6},{6,8},{8,10},{10,12},{12,14},{14,16},{16,18},{18... | collective-permute-start | bytes 393224 | tf_op jit(solution)/shard_map/ppermute | solution.py:11
  52.4 2.7 collective-permute-done.1
  56.6 3.0 collective-permute-start.5
  63.8 3.4 %concatenate.6 = bf16[28,128,128]{2,0,1:T(8,128)(2,1)S(1)} concatenate(bf16[4,128,128]{2,0,1:T(4,128)(2,1)} %copy.48, bf16[4,128,128]{2,0,1:T(4,128)(2,1)} %copy.49, bf16[4,128,128]{2,0,1:T(4,128)(2,1)S(1)} %copy.50, bf16[4,128,128]{2,0,1:T(4,128)(2,1)S(1)} %copy.51, bf16[4,128,128]{2,0,1:T(4,128)(2,1)S(1)} %copy.52, bf16[4,128,128]{2,0,1:T(4,128)(2,1)} %copy.53, ...), dimensions={0} | concatenate | bytes 1835008 | tf_op jit(solution)/shard_map/concatenate | solution.py:49
  67.2 4.0 %fusion.16 = (bf16[4,128,512]{2,0,1:T(4,128)(2,1)}, bf16[4,128,512]{2,0,1:T(4,128)(2,1)S(1)}) fusion(f32[28,128,512]{2,0,1:T(8,128)} %get-tuple-element.16, bf16[4,128,512]{2,0,1:T(4,128)(2,1)} %collective-permute-done.12, bf16[4,128,512]{2,0,1:T(4,128)(2,1)} %collective-permute-done.15), kind=kLoop, calls=%fused_computation.19 | loop fusion | flops 1572864 | bytes 4194304 | tf_op jit(solution)/shard_map/convert_element_type | solution.py:27
  72.5 3.2 collective-permute-start.16
  77.2 5.7 %collective-permute-done.13 = bf16[4,128,512]{2,0,1:T(4,128)(2,1)S(1)} collective-permute-done((bf16[4,128,512]{2,0,1:T(4,128)(2,1)}, bf16[4,128,512]{2,0,1:T(4,128)(2,1)S(1)}, u32[]{:S(2)}, u32[]{:S(2)}) %collective-permute-start.13) | collective-permute-done | bytes 524320 | tf_op jit(solution)/shard_map/ppermute | solution.py:11
  82.8 4.0 %fusion.15 = (bf16[4,128,512]{2,0,1:T(4,128)(2,1)}, bf16[4,128,512]{2,0,1:T(4,128)(2,1)}) fusion(f32[28,128,512]{2,0,1:T(8,128)} %get-tuple-element.16, bf16[4,128,512]{2,0,1:T(4,128)(2,1)S(1)} %collective-permute-done.13, bf16[4,128,512]{2,0,1:T(4,128)(2,1)} %collective-permute-done.16), kind=kLoop, calls=%fused_computation.17 | loop fusion | flops 1572864 | bytes 4194304 | tf_op jit(solution)/shard_map/convert_element_type | solution.py:27
  86.8 4.9 %collective-permute-start.14 = (bf16[4,128,512]{2,0,1:T(4,128)(2,1)}, bf16[4,128,512]{2,0,1:T(4,128)(2,1)}, u32[]{:S(2)}, u32[]{:S(2)}) collective-permute-start(bf16[4,128,512]{2,0,1:T(4,128)(2,1)} %get-tuple-element.5), channel_id=1, source_target_pairs={{0,2},{2,4},{4,6},{6,8},{8,10},{10,12},{12,14},{14,16},{16,18},{18... | collective-permute-start | bytes 1572872 | tf_op jit(solution)/shard_map/ppermute | solution.py:11
  93.0 9.4 %all_gather.6 = bf16[512,512]{1,0:T(8,128)(2,1)S(1)} all-gather(bf16[256,512]{1,0:T(8,128)(2,1)S(1)} %get-tuple-element.13), channel_id=1, replica_groups=mesh['row'=16,'rep'=2] {'rep'}, dimensions={0}, use_global_device_ids=true | all-gather | bytes 786432 | tf_op jit(solution)/shard_map/all_gather | solution.py:35
  102.4 4.4 %collective-permute-start.9 = (bf16[512,512]{1,0:T(8,128)(2,1)S(1)}, bf16[512,512]{1,0:T(8,128)(2,1)S(1)}, u32[]{:S(2)}, u32[]{:S(2)}) collective-permute-start(bf16[512,512]{1,0:T(8,128)(2,1)S(1)} %all_gather.6), channel_id=1, source_target_pairs={{0,30},{2,0},{4,2},{6,4},{8,6},{10,8},{12,10},{14,12},{16,14},{18,... | collective-permute-start | bytes 1572872 | tf_op jit(solution)/shard_map/ppermute | solution.py:11
  106.9 2.3 fusion.17
  110.5 3.3 collective-permute-done.6
  114.2 4.1 %collective-permute-start.10 = (bf16[512,512]{1,0:T(8,128)(2,1)S(1)}, bf16[512,512]{1,0:T(8,128)(2,1)S(1)}, u32[]{:S(2)}, u32[]{:S(2)}) collective-permute-start(bf16[512,512]{1,0:T(8,128)(2,1)S(1)} %collective-permute-done.9), channel_id=1, source_target_pairs={{0,30},{2,0},{4,2},{6,4},{8,6},{10,8},{12,10},{14,12},{16,14},{18,... | collective-permute-start | bytes 1572872 | tf_op jit(solution)/shard_map/ppermute | solution.py:11
  118.3 7.0 %collective-permute-done.7 = bf16[512,512]{1,0:T(8,128)(2,1)S(1)} collective-permute-done((bf16[512,512]{1,0:T(8,128)(2,1)S(1)}, bf16[512,512]{1,0:T(8,128)(2,1)S(1)}, u32[]{:S(2)}, u32[]{:S(2)}) %collective-permute-start.7) | collective-permute-done | bytes 524320 | tf_op jit(solution)/shard_map/ppermute | solution.py:11
  125.2 2.4 collective-permute-start.8
  127.6 2.0 collective-permute-start.11
  134.4 2.3 collective-permute-done.8
  139.0 18.7 %concatenate.7 = bf16[28,128,512]{2,0,1:T(8,128)(2,1)} concatenate(bf16[4,128,512]{2,0,1:T(4,128)(2,1)} %copy.56, bf16[4,128,512]{2,0,1:T(4,128)(2,1)} %copy.57, bf16[4,128,512]{2,0,1:T(4,128)(2,1)S(1)} %copy.58, bf16[4,128,512]{2,0,1:T(4,128)(2,1)S(1)} %copy.59, bf16[4,128,512]{2,0,1:T(4,128)(2,1)S(1)} %copy.60, bf16[4,128,512]{2,0,1:T(4,128)(2,1)} %copy.61, ...), dimensions={0} | concatenate | bytes 7340032 | tf_op jit(solution)/shard_map/concatenate | solution.py:49
  157.7 3.1 fusion.9
  160.8 1.6 fusion.7
  162.6 2.0 fusion.21
  164.5 25.6 %reduce-scatter.6.cloned.1.call-done = f32[256,512]{1,0:T(8,128)} async-done(((f32[512,512]{1,0:T(8,128)}), f32[256,512]{1,0:T(8,128)}) %reduce-scatter.6.cloned.1.call-update) | async-done | bytes 524304 | tf_op jit(solution)/shard_map/reduce_scatter | solution.py:31
  193.7 135.1 %all-reduce.4.cloned.1.call-done = (f32[128,512]{1,0:T(8,128)}, f32[512,512]{1,0:T(8,128)}) async-done(((f32[128,512]{1,0:T(8,128)}, f32[512,512]{1,0:T(8,128)}), (f32[128,512]{1,0:T(8,128)}, f32[512,512]{1,0:T(8,128)})) %all-reduce.4.cloned.1.call-update) | async-done | bytes 1310736 | tf_op jit(solution)/shard_map/psum | solution.py:140
  328.8 1.7 copy.85
  330.4 2.3 copy.86
  (89 shorter events, 30.1 us)
Async XLA Ops:
  7.2 11.2 %copy-start = (bf16[512,512]{1,0:T(8,128)(2,1)S(1)}, bf16[512,512]{1,0:T(8,128)(2,1)}, u32[]{:S(2)}) copy-start(bf16[512,512]{1,0:T(8,128)(2,1)} %param.9) | copy-start | bytes 1572868
  7.2 20.4 %copy-start.1 = (bf16[4,4,128,128]{3,2,1,0:T(8,128)(2,1)S(1)}, bf16[4,4,128,128]{3,2,1,0:T(8,128)(2,1)}, u32[]{:S(2)}) copy-start(bf16[4,4,128,128]{3,2,1,0:T(8,128)(2,1)} %param.11) | copy-start | bytes 1572868
  7.2 84.6 %reduce-scatter.4.cloned.1.call-start = ((), (), s32[]{:S(2)}) async-start(), calls=%async_computation.3 | async-start | bytes 393216 | tf_op jit(solution)/shard_map/reduce_scatter | solution.py:31
  18.4 9.2 %copy-start.9 = (f32[256]{0:T(256)}, f32[256]{0:T(256)S(1)}, u32[]{:S(2)}) copy-start(f32[256]{0:T(256)S(1)} %dynamic-slice_add_fusion) | copy-start | bytes 3076
  19.7 7.9 %copy-start.2 = (bf16[256,512]{1,0:T(8,128)(2,1)}, bf16[256,512]{1,0:T(8,128)(2,1)S(1)}, u32[]{:S(2)}) copy-start(bf16[256,512]{1,0:T(8,128)(2,1)S(1)} %fusion.12) | copy-start | bytes 786436
  28.5 11.1 %copy-start.5 = (bf16[512,128]{1,0:T(8,128)(2,1)S(1)}, bf16[512,128]{1,0:T(8,128)(2,1)}, u32[]{:S(2)}) copy-start(bf16[512,128]{1,0:T(8,128)(2,1)} %param.7) | copy-start | bytes 393220
  35.1 32.1 %collective-permute-start.12 = (bf16[4,128,512]{2,0,1:T(4,128)(2,1)S(1)}, bf16[4,128,512]{2,0,1:T(4,128)(2,1)}, u32[]{:S(2)}, u32[]{:S(2)}) collective-permute-start(bf16[4,128,512]{2,0,1:T(4,128)(2,1)S(1)} %get-tuple-element.9), channel_id=1, source_target_pairs={{0,2},{2,4},{4,6},{6,8},{8,10},{10,12},{12,14},{14,16},{16,18},{18... | collective-permute-start | bytes 1572872 | tf_op jit(solution)/shard_map/ppermute | solution.py:11
  35.2 32.0 %collective-permute-start.15 = (bf16[4,128,512]{2,0,1:T(4,128)(2,1)S(1)}, bf16[4,128,512]{2,0,1:T(4,128)(2,1)}, u32[]{:S(2)}, u32[]{:S(2)}) collective-permute-start(bf16[4,128,512]{2,0,1:T(4,128)(2,1)S(1)} %get-tuple-element.10), channel_id=1, source_target_pairs={{0,30},{2,0},{4,2},{6,4},{8,6},{10,8},{12,10},{14,12},{16,14},{18,... | collective-permute-start | bytes 1572872 | tf_op jit(solution)/shard_map/ppermute | solution.py:11
  39.6 8.4 %collective-permute-start = (bf16[512,128]{1,0:T(8,128)(2,1)S(1)}, bf16[512,128]{1,0:T(8,128)(2,1)S(1)}, u32[]{:S(2)}, u32[]{:S(2)}) collective-permute-start(bf16[512,128]{1,0:T(8,128)(2,1)S(1)} %copy-done.5), channel_id=1, source_target_pairs={{0,2},{2,4},{4,6},{6,8},{8,10},{10,12},{12,14},{14,16},{16,18},{18... | collective-permute-start | bytes 393224 | tf_op jit(solution)/shard_map/ppermute | solution.py:11
  39.6 12.0 %collective-permute-start.3 = (bf16[512,128]{1,0:T(8,128)(2,1)S(1)}, bf16[512,128]{1,0:T(8,128)(2,1)S(1)}, u32[]{:S(2)}, u32[]{:S(2)}) collective-permute-start(bf16[512,128]{1,0:T(8,128)(2,1)S(1)} %copy-done.5), channel_id=1, source_target_pairs={{0,30},{2,0},{4,2},{6,4},{8,6},{10,8},{12,10},{14,12},{16,14},{18,... | collective-permute-start | bytes 393224 | tf_op jit(solution)/shard_map/ppermute | solution.py:11
  48.0 7.2 %collective-permute-start.1 = (bf16[512,128]{1,0:T(8,128)(2,1)S(1)}, bf16[512,128]{1,0:T(8,128)(2,1)S(1)}, u32[]{:S(2)}, u32[]{:S(2)}) collective-permute-start(bf16[512,128]{1,0:T(8,128)(2,1)S(1)} %collective-permute-done), channel_id=1, source_target_pairs={{0,2},{2,4},{4,6},{6,8},{8,10},{10,12},{12,14},{14,16},{16,18},{18... | collective-permute-start | bytes 393224 | tf_op jit(solution)/shard_map/ppermute | solution.py:11
  51.6 5.0 %collective-permute-start.4 = (bf16[512,128]{1,0:T(8,128)(2,1)S(1)}, bf16[512,128]{1,0:T(8,128)(2,1)S(1)}, u32[]{:S(2)}, u32[]{:S(2)}) collective-permute-start(bf16[512,128]{1,0:T(8,128)(2,1)S(1)} %collective-permute-done.3), channel_id=1, source_target_pairs={{0,30},{2,0},{4,2},{6,4},{8,6},{10,8},{12,10},{14,12},{16,14},{18,... | collective-permute-start | bytes 393224 | tf_op jit(solution)/shard_map/ppermute | solution.py:11
  55.2 7.1 %collective-permute-start.2 = (bf16[512,128]{1,0:T(8,128)(2,1)S(1)}, bf16[512,128]{1,0:T(8,128)(2,1)S(1)}, u32[]{:S(2)}, u32[]{:S(2)}) collective-permute-start(bf16[512,128]{1,0:T(8,128)(2,1)S(1)} %collective-permute-done.1), channel_id=1, source_target_pairs={{0,2},{2,4},{4,6},{6,8},{8,10},{10,12},{12,14},{14,16},{16,18},{18... | collective-permute-start | bytes 393224 | tf_op jit(solution)/shard_map/ppermute | solution.py:11
  56.6 6.4 %collective-permute-start.5 = (bf16[512,128]{1,0:T(8,128)(2,1)S(1)}, bf16[512,128]{1,0:T(8,128)(2,1)S(1)}, u32[]{:S(2)}, u32[]{:S(2)}) collective-permute-start(bf16[512,128]{1,0:T(8,128)(2,1)S(1)} %collective-permute-done.4), channel_id=1, source_target_pairs={{0,30},{2,0},{4,2},{6,4},{8,6},{10,8},{12,10},{14,12},{16,14},{18,... | collective-permute-start | bytes 393224 | tf_op jit(solution)/shard_map/ppermute | solution.py:11
  71.2 20.6 %copy-start.6 = (bf16[512,128]{1,0:T(8,128)(2,1)S(1)}, bf16[512,128]{1,0:T(8,128)(2,1)}, u32[]{:S(2)}) copy-start(bf16[512,128]{1,0:T(8,128)(2,1)} %param.7) | copy-start | bytes 393220
  71.2 20.6 %copy-start.10 = (f32[256]{0:T(256)S(1)}, f32[256]{0:T(256)}, u32[]{:S(2)}) copy-start(f32[256]{0:T(256)} %copy-done.9) | copy-start | bytes 3076
  71.2 21.6 %copy-start.8 = (bf16[128,512]{1,0:T(8,128)(2,1)S(1)}, bf16[128,512]{1,0:T(8,128)(2,1)}, u32[]{:S(2)}) copy-start(bf16[128,512]{1,0:T(8,128)(2,1)} %param.8) | copy-start | bytes 393220
  71.2 11.7 %collective-permute-start.13 = (bf16[4,128,512]{2,0,1:T(4,128)(2,1)}, bf16[4,128,512]{2,0,1:T(4,128)(2,1)S(1)}, u32[]{:S(2)}, u32[]{:S(2)}) collective-permute-start(bf16[4,128,512]{2,0,1:T(4,128)(2,1)} %get-tuple-element.7), channel_id=1, source_target_pairs={{0,2},{2,4},{4,6},{6,8},{8,10},{10,12},{12,14},{14,16},{16,18},{18... | collective-permute-start | bytes 1572872 | tf_op jit(solution)/shard_map/ppermute | solution.py:11
  72.5 10.4 %collective-permute-start.16 = (bf16[4,128,512]{2,0,1:T(4,128)(2,1)S(1)}, bf16[4,128,512]{2,0,1:T(4,128)(2,1)}, u32[]{:S(2)}, u32[]{:S(2)}) collective-permute-start(bf16[4,128,512]{2,0,1:T(4,128)(2,1)S(1)} %get-tuple-element.8), channel_id=1, source_target_pairs={{0,30},{2,0},{4,2},{6,4},{8,6},{10,8},{12,10},{14,12},{16,14},{18,... | collective-permute-start | bytes 1572872 | tf_op jit(solution)/shard_map/ppermute | solution.py:11
  77.1 85.4 %reduce-scatter.8.cloned.1.call-start = ((), (), s32[]{:S(2)}) async-start(), calls=%async_computation.5 | async-start | bytes 1572864 | tf_op jit(solution)/shard_map/reduce_scatter | solution.py:31
  86.8 20.0 %collective-permute-start.14 = (bf16[4,128,512]{2,0,1:T(4,128)(2,1)}, bf16[4,128,512]{2,0,1:T(4,128)(2,1)}, u32[]{:S(2)}, u32[]{:S(2)}) collective-permute-start(bf16[4,128,512]{2,0,1:T(4,128)(2,1)} %get-tuple-element.5), channel_id=1, source_target_pairs={{0,2},{2,4},{4,6},{6,8},{8,10},{10,12},{12,14},{14,16},{16,18},{18... | collective-permute-start | bytes 1572872 | tf_op jit(solution)/shard_map/ppermute | solution.py:11
  91.8 15.1 %collective-permute-start.17 = (bf16[4,128,512]{2,0,1:T(4,128)(2,1)}, bf16[4,128,512]{2,0,1:T(4,128)(2,1)}, u32[]{:S(2)}, u32[]{:S(2)}) collective-permute-start(bf16[4,128,512]{2,0,1:T(4,128)(2,1)} %get-tuple-element.6), channel_id=1, source_target_pairs={{0,30},{2,0},{4,2},{6,4},{8,6},{10,8},{12,10},{14,12},{16,14},{18,... | collective-permute-start | bytes 1572872 | tf_op jit(solution)/shard_map/ppermute | solution.py:11
  102.4 11.4 %collective-permute-start.6 = (bf16[512,512]{1,0:T(8,128)(2,1)S(1)}, bf16[512,512]{1,0:T(8,128)(2,1)S(1)}, u32[]{:S(2)}, u32[]{:S(2)}) collective-permute-start(bf16[512,512]{1,0:T(8,128)(2,1)S(1)} %all_gather.6), channel_id=1, source_target_pairs={{0,2},{2,4},{4,6},{6,8},{8,10},{10,12},{12,14},{14,16},{16,18},{18... | collective-permute-start | bytes 1572872 | tf_op jit(solution)/shard_map/ppermute | solution.py:11
  102.4 11.8 %collective-permute-start.9 = (bf16[512,512]{1,0:T(8,128)(2,1)S(1)}, bf16[512,512]{1,0:T(8,128)(2,1)S(1)}, u32[]{:S(2)}, u32[]{:S(2)}) collective-permute-start(bf16[512,512]{1,0:T(8,128)(2,1)S(1)} %all_gather.6), channel_id=1, source_target_pairs={{0,30},{2,0},{4,2},{6,4},{8,6},{10,8},{12,10},{14,12},{16,14},{18,... | collective-permute-start | bytes 1572872 | tf_op jit(solution)/shard_map/ppermute | solution.py:11
  110.4 79.7 %reduce-scatter.6.cloned.1.call-start = ((), (), s32[]{:S(2)}) async-start(), calls=%async_computation.4 | async-start | bytes 1572864 | tf_op jit(solution)/shard_map/reduce_scatter | solution.py:31
  113.8 11.4 %collective-permute-start.7 = (bf16[512,512]{1,0:T(8,128)(2,1)S(1)}, bf16[512,512]{1,0:T(8,128)(2,1)S(1)}, u32[]{:S(2)}, u32[]{:S(2)}) collective-permute-start(bf16[512,512]{1,0:T(8,128)(2,1)S(1)} %collective-permute-done.6), channel_id=1, source_target_pairs={{0,2},{2,4},{4,6},{6,8},{8,10},{10,12},{12,14},{14,16},{16,18},{18... | collective-permute-start | bytes 1572872 | tf_op jit(solution)/shard_map/ppermute | solution.py:11
  114.2 15.5 %copy-start.4 = (bf16[512,512]{1,0:T(8,128)(2,1)}, bf16[512,512]{1,0:T(8,128)(2,1)S(1)}, u32[]{:S(2)}) copy-start(bf16[512,512]{1,0:T(8,128)(2,1)S(1)} %collective-permute-done.9) | copy-start | bytes 1572868
  114.2 13.4 %collective-permute-start.10 = (bf16[512,512]{1,0:T(8,128)(2,1)S(1)}, bf16[512,512]{1,0:T(8,128)(2,1)S(1)}, u32[]{:S(2)}, u32[]{:S(2)}) collective-permute-start(bf16[512,512]{1,0:T(8,128)(2,1)S(1)} %collective-permute-done.9), channel_id=1, source_target_pairs={{0,30},{2,0},{4,2},{6,4},{8,6},{10,8},{12,10},{14,12},{16,14},{18,... | collective-permute-start | bytes 1572872 | tf_op jit(solution)/shard_map/ppermute | solution.py:11
  125.2 11.4 %collective-permute-start.8 = (bf16[512,512]{1,0:T(8,128)(2,1)S(1)}, bf16[512,512]{1,0:T(8,128)(2,1)S(1)}, u32[]{:S(2)}, u32[]{:S(2)}) collective-permute-start(bf16[512,512]{1,0:T(8,128)(2,1)S(1)} %collective-permute-done.7), channel_id=1, source_target_pairs={{0,2},{2,4},{4,6},{6,8},{8,10},{10,12},{12,14},{14,16},{16,18},{18... | collective-permute-start | bytes 1572872 | tf_op jit(solution)/shard_map/ppermute | solution.py:11
  127.6 10.2 %collective-permute-start.11 = (bf16[512,512]{1,0:T(8,128)(2,1)S(1)}, bf16[512,512]{1,0:T(8,128)(2,1)S(1)}, u32[]{:S(2)}, u32[]{:S(2)}) collective-permute-start(bf16[512,512]{1,0:T(8,128)(2,1)S(1)} %collective-permute-done.10), channel_id=1, source_target_pairs={{0,30},{2,0},{4,2},{6,4},{8,6},{10,8},{12,10},{14,12},{16,14},{18,... | collective-permute-start | bytes 1572872 | tf_op jit(solution)/shard_map/ppermute | solution.py:11
  160.8 30.5 %copy-start.7 = (bf16[256,512]{1,0:T(8,128)(2,1)S(1)}, bf16[256,512]{1,0:T(8,128)(2,1)}, u32[]{:S(2)}) copy-start(bf16[256,512]{1,0:T(8,128)(2,1)} %param.10) | copy-start | bytes 786436
  162.5 166.3 %all-reduce.4.cloned.1.call-start = ((), (), s32[]{:S(2)}) async-start(), calls=%async_computation.6 | async-start | bytes 2621440 | tf_op jit(solution)/shard_map/psum | solution.py:140
  (1 other events, 1.8 us)
Sparse Core Ops, SparseCore 0:
  77.2 9.7 reduce-scatter.3
  110.6 18.2 reduce-scatter.7
  162.6 27.5 reduce-scatter.5
  197.2 131.5 all-reduce.3
where the time goes:
time: 341 us; the launch traced here: 339 us
  waiting for transfers between devices  187 us (55%)
  starting transfers between devices  40.7 us (12%)
  local copies, waits for them, and re-layouts  40 us (12%)
  blocking collectives  23.1 us (7%)
  matrix products  19.1 us (6%)
  other arithmetic  15 us (4%)
  between operations  14.7 us (4%)
    psum x1, waiting for transfers between devices, body(): lax.psum((grad_input, grad_output), ('row', 'rep'))  135 us
    ppermute x18, starting transfers between devices, passed_along(): lax.ppermute(shard, axis, [(i, (i + by) % peers) for i in range(peers)])  40.6 us
    ppermute x18, waiting for transfers between devices, passed_along(): lax.ppermute(shard, axis, [(i, (i + by) % peers) for i in range(peers)])  25.7 us
    reduce_scatter x3, waiting for transfers between devices, rep_reduce(): return lax.psum_scatter(parts, 'rep', scatter_dimension=0, tiled=True)  25.7 us
    concatenate x2, local copies, waits for them, and re-layouts, band_stack(): jnp.concatenate([held_by[shift].reshape(blocks, tile, -1) for shift in ra...  22.1 us
    all_gather x2, blocking collectives, share_rows(): return lax.all_gather(value, 'rep', axis=0, tiled=True)  17.3 us
    reshape x14, local copies, waits for them, and re-layouts, band_stack(): held_by[shift].reshape(blocks, tile, -1)  10.4 us
    convert_element_type x2, other arithmetic, move_terms(): value.astype(jnp.bfloat16)  7.95 us
  transfers between devices with their start and end apart: 22, of which 9 were waited for; matrix products, arithmetic and copies ran while one was open for 15% of the time, Pallas kernels for 0%

commit v1 on v0

v1 whole, which is shorter than its diff:
```python
import functools

import jax
import jax.numpy as jnp
from jax import lax
from jax.experimental import pallas as pl
from jax.experimental.pallas import tpu as pltpu
from jax.sharding import PartitionSpec as P

HOPS = 3
SPAN = 2 * HOPS + 1
SHIFTS = [s for s in range(-HOPS, HOPS + 1) if s]
MESH = pl.DeviceIdType.MESH
ANY = pl.BlockSpec(memory_space=pl.ANY)
VMEM = pl.BlockSpec(memory_space=pltpu.VMEM)
SMEM = pl.BlockSpec(memory_space=pltpu.SMEM)
F32 = jnp.float32
BF16 = jnp.bfloat16


def dot(a, b, dims):
    return lax.dot_general(a, b, ((dims[:1], dims[1:]), ((), ())), preferred_element_type=F32)


def greet(peers):
    barrier = pltpu.get_barrier_semaphore()
    for peer in peers:
        pl.semaphore_signal(barrier, inc=1, device_id=peer, device_id_type=MESH)
    pl.semaphore_wait(barrier, len(peers))


def remote(src, dst, send, recv, index, peer):
    return pltpu.make_async_remote_copy(
        src_ref=src, dst_ref=dst, send_sem=send.at[index], recv_sem=recv.at[index],
        device_id=peer, device_id_type=MESH,
    )


def open_kernel(rows, reps, feats, cot, tiles, cols, band, cots, all_tiles, all_cols, send, recv, local):
    row, rep = lax.axis_index("row"), lax.axis_index("rep")
    near = [(lax.rem(row + s + rows, rows), rep) for s in SHIFTS]
    others = [(row, lax.rem(rep + t, reps)) for t in range(1, reps)]
    greet(near + others)
    copies, n = [], 0
    pieces = ((tiles, all_tiles), (cols, all_cols), (cot, cots))
    for peer in others:
        for src, dst in pieces:
            copies.append(remote(src, dst.at[rep], send, recv, n, peer))
            n += 1
    for s, peer in zip(SHIFTS, near):
        copies.append(remote(feats, band.at[HOPS - s], send, recv, n, peer))
        n += 1
    for i, (src, dst) in enumerate(pieces):
        copies.append(pltpu.make_async_copy(src, dst.at[rep], local.at[i]))
    copies.append(pltpu.make_async_copy(feats, band.at[HOPS], local.at[3]))
    for copy in copies:
        copy.start()
    for copy in copies:
        copy.wait()


def front_kernel(rows, reps, blocks, tile, tiles, cols, row_ids, band_ids, band, cots, w1, w2,
                 dense, first_o, preact_o, hidden_o, scaled_o, terms_o, own_o, deg_o):
    row, rep = lax.axis_index("row"), lax.axis_index("rep")
    total = rows * blocks
    per = tiles.shape[2]
    dense[...] = jnp.zeros_like(dense)
    for b in range(blocks):
        at = pl.ds(b * tile, tile)
        ids = row_ids[at, :]
        sums = jnp.ones((tile, 1), F32)
        for j in range(reps):
            for k in range(per):
                slot = lax.rem(cols[j, b, k] + total - (row - HOPS) * blocks, total)
                same = ids == band_ids[pl.ds(slot, 1), :]
                value = jnp.where(same, tiles[j, b, k].astype(F32), 0.0)
                sums = sums + jnp.sum(value, axis=1, keepdims=True)
                dense[at, pl.ds(pl.multiple_of(slot * tile, tile), tile)] = value.astype(BF16)
        deg_o[at, :] = sums
    degree = deg_o[...]
    local = blocks * tile
    flat = band[...].reshape(SPAN * local, -1)
    summed = dot(dense[...], flat, (1, 0))
    first = ((summed + band[HOPS].astype(F32)) / degree).astype(BF16)
    first_o[...] = first
    half = w1.shape[1] // reps
    at = pl.ds(pl.multiple_of(rep * half, half), half)
    preact = dot(first, w1[:, at], (1, 0))
    preact_o[...] = preact
    hidden_o[...] = jnp.maximum(preact, 0.0).astype(BF16)
    pulled = dot(cots[...].reshape(local, -1), w2[at, :], (1, 1))
    scaled = (pulled / degree).astype(BF16)
    scaled_t = scaled.astype(F32).T.astype(BF16)
    for s in range(SPAN):
        part = dot(scaled_t, dense[:, s * local:(s + 1) * local], (1, 0))
        if s == HOPS:
            own_o[...] = part.T + scaled.astype(F32)
        terms_o[s] = part.astype(BF16)
    scaled_o[...] = scaled


def band_kernel(rows, hidden, terms, hid_band, term_band, send, recv, local):
    row, rep = lax.axis_index("row"), lax.axis_index("rep")
    near = [(lax.rem(row + s + rows, rows), rep) for s in SHIFTS]
    greet(near)
    copies, n = [], 0
    for s, peer in zip(SHIFTS, near):
        copies.append(remote(hidden, hid_band.at[HOPS - s], send, recv, n, peer))
        where = (HOPS - s) if s > 0 else (HOPS - s - 1)
        copies.append(remote(terms.at[HOPS + s], term_band.at[where], send, recv, n + 1, peer))
        n += 2
    copies.append(pltpu.make_async_copy(hidden, hid_band.at[HOPS], local.at[0]))
    for copy in copies:
        copy.start()
    for copy in copies:
        copy.wait()


def back_kernel(dense, hid_band, term_band, first, preact, own, deg, cots, second_o, grads_o):
    local, half = preact.shape
    summed = dot(dense[...], hid_band[...].reshape(SPAN * local, half), (1, 0))
    second = ((summed + hid_band[HOPS].astype(F32)) / deg[...]).astype(BF16)
    second_o[...] = second
    out = dot(second, cots[...].reshape(local, -1), (0, 0))
    width = out.shape[1] // half
    for i in range(width):
        grads_o[i * half:(i + 1) * half, :] = out[:, i * half:(i + 1) * half]
    got = term_band[0].astype(F32)
    for i in range(1, SPAN - 1):
        got = got + term_band[i].astype(F32)
    back = got.T + own[...]
    delta = jnp.where(preact[...] > 0.0, back, 0.0).astype(BF16)
    grads_o[width * half:, :] = dot(first[...], delta, (0, 0))


def swap_kernel(reps, second, full, send, recv, local):
    row, rep = lax.axis_index("row"), lax.axis_index("rep")
    others = [(row, lax.rem(rep + t, reps)) for t in range(1, reps)]
    greet(others)
    copies = [remote(second.at[peer[1]], full.at[rep], send, recv, n, peer) for n, peer in enumerate(others)]
    copies.append(pltpu.make_async_copy(second.at[rep], full.at[rep], local.at[0]))
    for copy in copies:
        copy.start()
    for copy in copies:
        copy.wait()


def sum_kernel(chips, reps, second, grads, full, whole, mine, pair, parts, send, recv, local):
    row, rep = lax.axis_index("row"), lax.axis_index("rep")
    chip, core = row // 2, lax.rem(row, 2)
    sibling = (chip * 2 + 1 - core, rep)
    turns = [lax.rem(chip + t, chips) for t in range(1, chips)]
    peers = [(q * 2 + core, rep) for q in turns]
    others = [(row, lax.rem(rep + t, reps)) for t in range(1, reps)]
    greet([sibling] + peers + others)
    a = remote(grads.at[1 - core], pair, send, recv, 0, sibling)
    a.start()
    early = [remote(second.at[peer[1]], full.at[rep], send, recv, 1 + n, peer) for n, peer in enumerate(others)]
    early.append(pltpu.make_async_copy(second.at[rep], full.at[rep], local.at[0]))
    for copy in early:
        copy.start()
    base = reps
    a.wait()
    mine[...] = grads[core] + pair[...]
    copies = [remote(mine.at[q], parts.at[t], send, recv, base + t, peer)
              for t, (q, peer) in enumerate(zip(turns, peers))]
    for copy in copies:
        copy.start()
    total = mine[chip]
    for t, copy in enumerate(copies):
        copy.wait_recv()
        total = total + parts[t]
    whole[rep, core, chip] = total
    base = base + chips - 1
    spread = [remote(whole.at[rep, core, chip], whole.at[rep, core, chip], send, recv, base + t, peer)
              for t, peer in enumerate(peers)]
    for copy in spread:
        copy.start()
    for copy in copies:
        copy.wait_send()
    for copy in spread:
        copy.wait()
    base = base + chips - 1
    block = whole.at[rep, core]
    last = [remote(block, block, send, recv, base + n, peer) for n, peer in enumerate(others)]
    base = base + reps - 1
    side = [remote(block, block, send, recv, base, sibling)]
    for copy in last + side:
        copy.start()
    for n, copy in enumerate(last):
        copy.wait_recv()
        came = whole.at[lax.rem(rep + reps - 1 - n, reps), core]
        step = remote(came, came, send, recv, base + 1 + n, sibling)
        step.start()
        side.append(step)
    for copy in last:
        copy.wait_send()
    for copy in side + early:
        copy.wait()


def params(number=None):
    limit = 48 << 20
    if number is None:
        return pltpu.CompilerParams(vmem_limit_bytes=limit)
    return pltpu.CompilerParams(vmem_limit_bytes=limit, collective_id=number, has_side_effects=True)


def shape(dims, kind):
    return jax.ShapeDtypeStruct(dims, kind)


def sems(count):
    return [pltpu.SemaphoreType.DMA((count,)), pltpu.SemaphoreType.DMA((count,)), pltpu.SemaphoreType.DMA((4,))]


def body(
    features, input_weight, output_weight, cotangent, adjacency_tiles, block_columns, graph_sizes
):
    row = lax.axis_index("row")
    rows, reps = lax.axis_size("row"), lax.axis_size("rep")
    blocks, per, tile = adjacency_tiles.shape[:3]
    local = blocks * tile
    fin = features.shape[1]
    hid = output_weight.shape[0]
    half, quarter = hid // reps, local // reps
    nodes = rows * local
    ends = jnp.cumsum(graph_sizes)

    def graph_of(places):
        return jnp.sum((places[..., None] >= ends).astype(jnp.int32), axis=-1)

    spots = lax.rem((row - HOPS) * local + nodes + jnp.arange(SPAN * local, dtype=jnp.int32), nodes)
    ids = graph_of(spots)
    row_ids = ids[HOPS * local:(HOPS + 1) * local].reshape(local, 1)
    band_ids = ids.reshape(SPAN * blocks, tile)
    padded = jnp.pad(block_columns, ((0, 8 - blocks), (0, 128 - per)))
    band, cots, all_tiles, all_cols = pl.pallas_call(
        functools.partial(open_kernel, rows, reps),
        out_shape=(
            shape((SPAN, local, fin), BF16),
            shape((reps, quarter, hid), BF16),
            shape((reps,) + adjacency_tiles.shape, BF16),
            shape((reps, 8, 128), jnp.int32),
        ),
        in_specs=[ANY] * 4,
        out_specs=(ANY,) * 4,
        scratch_shapes=sems(3 * (reps - 1) + 2 * HOPS),
        compiler_params=params(0),
    )(features, cotangent, adjacency_tiles, padded)
    dense, first, preact, hidden, scaled, terms, own, degree = pl.pallas_call(
        functools.partial(front_kernel, rows, reps, blocks, tile),
        out_shape=(
            shape((local, SPAN * local), BF16),
            shape((local, fin), BF16),
            shape((local, half), F32),
            shape((local, half), BF16),
            shape((local, half), BF16),
            shape((SPAN, half, local), BF16),
            shape((local, half), F32),
            shape((local, 1), F32),
        ),
        in_specs=[VMEM, SMEM] + [VMEM] * 6,
        out_specs=(VMEM,) * 8,
        compiler_params=params(),
    )(all_tiles, all_cols, row_ids, band_ids, band, cots, input_weight, output_weight)
    hid_band, term_band = pl.pallas_call(
        functools.partial(band_kernel, rows),
        out_shape=(shape((SPAN, local, half), BF16), shape((SPAN - 1, half, local), BF16)),
        in_specs=[ANY] * 2,
        out_specs=(ANY,) * 2,
        scratch_shapes=sems(4 * HOPS),
        compiler_params=params(1),
    )(hidden, terms)
    tall = hid * hid // reps // half + fin
    second, grads = pl.pallas_call(
        back_kernel,
        out_shape=(shape((local, half), BF16), shape((tall, half), F32)),
        in_specs=[VMEM] * 8,
        out_specs=(VMEM,) * 2,
        compiler_params=params(),
    )(dense, hid_band, term_band, first, preact, own, degree, cots)
    second = second.reshape(reps, quarter, half)
    if rows <= 16 and rows % 2 == 0 and tall % (8 * rows) == 0:
        chips = rows // 2
        chunk = tall // rows
        full, whole = pl.pallas_call(
            functools.partial(sum_kernel, chips, reps),
            out_shape=(shape((reps, quarter, half), BF16), shape((reps, 2, chips, chunk, half), F32)),
            in_specs=[ANY, VMEM],
            out_specs=(ANY, VMEM),
            scratch_shapes=[
                pltpu.VMEM((chips, chunk, half), F32),
                pltpu.VMEM((chips, chunk, half), F32),
                pltpu.VMEM((chips - 1, chunk, half), F32),
            ] + sems(3 * reps + 2 * chips),
            compiler_params=params(2),
        )(second, grads.reshape(2, chips, chunk, half))
        whole = whole.reshape(reps, tall, half)
    else:
        full = pl.pallas_call(
            functools.partial(swap_kernel, reps),
            out_shape=shape((reps, quarter, half), BF16),
            in_specs=[ANY],
            out_specs=ANY,
            scratch_shapes=sems(reps),
            compiler_params=params(2),
        )(second)
        whole = lax.all_gather(lax.psum(grads, "row"), "rep", axis=0)
    scores = dot(full.transpose(1, 0, 2).reshape(quarter, hid), output_weight, (1, 0)).astype(BF16)
    grad_input = whole[:, tall - fin:].transpose(1, 0, 2).reshape(fin, hid)
    grad_output = whole[:, :tall - fin].reshape(reps, hid // half, half, half)
    grad_output = grad_output.transpose(0, 2, 1, 3).reshape(hid, hid)
    return scores, grad_input, grad_output


def solution(mesh):
    placed = (
        P("row", None),
        P(),
        P(),
        P(("row", "rep"), None),
        P("row", "rep", None, None),
        P("row", "rep"),
        P(),
    )
    return jax.shard_map(
        body,
        mesh=mesh,
        in_specs=placed,
        out_specs=(P(("row", "rep"), None), P(), P()),
        check_vma=False,
    )
```

time: 341 us -> 127 us (0.37)
  waiting for transfers between devices: 187 us -> 0 us
  Pallas kernels: 0 us -> 111 us
  starting transfers between devices: 40.7 us -> 0 us
  local copies, waits for them, and re-layouts: 40 us -> 11.9 us
  blocking collectives: 23.1 us -> 0 us
  matrix products: 19.1 us -> 1.03 us
  other arithmetic: 15 us -> 0.28 us
  between operations: 14.7 us -> 0.75 us
    psum x1 -> x0, waiting for transfers between devices: 135 us -> none  [body(): lax.psum((grad_input, grad_output), ('row', 'rep'))]
    pallas_call x0 -> x5, Pallas kernels: none -> 111 us  [the longest x1 45.3 us: body(): pl.pallas_call(functools.partial(band_kernel, rows), out_shape=(shape((SP...]
    ppermute x18 -> x0, starting transfers between devices: 40.6 us -> none  [passed_along(): lax.ppermute(shard, axis, [(i, (i + by) % peers) for i in range(peers)])]
    ppermute x18 -> x0, waiting for transfers between devices: 25.7 us -> none  [passed_along(): lax.ppermute(shard, axis, [(i, (i + by) % peers) for i in range(peers)])]
    reduce_scatter x3 -> x0, waiting for transfers between devices: 25.7 us -> none  [rep_reduce(): return lax.psum_scatter(parts, 'rep', scatter_dimension=0, tiled=True)]
    concatenate x2 -> x0, local copies, waits for them, and re-layouts: 22.1 us -> none  [band_stack(): jnp.concatenate([held_by[shift].reshape(blocks, tile, -1) for shift in ra...]
    dot_general x11 -> x1, matrix products: 19.1 us -> 1.03 us  [dot(): lax.dot_general(a, b, ((dims[:1], dims[1:]), ((), ())), preferred_element...]
    all_gather x2 -> x0, blocking collectives: 17.3 us -> none  [share_rows(): return lax.all_gather(value, 'rep', axis=0, tiled=True)]
  transfers between devices with their start and end apart: 22 -> 0, of which waited for: 9 -> 0; matrix products, arithmetic and copies ran while one was open for 15% -> 0% of each run, Pallas kernels for 0% -> 0%
where the time goes in v1:
time: 127 us; the launch traced here: 125 us
  Pallas kernels  111 us (87%)
  local copies, waits for them, and re-layouts  11.9 us (9%)
    pallas_call x1, Pallas kernels, body(): pl.pallas_call(functools.partial(band_kernel, rows), out_shape=(shape((SP...  45.3 us
    pallas_call x1, Pallas kernels, body(): pl.pallas_call(functools.partial(sum_kernel, chips, reps), out_shape=(sha...  28.4 us
    pallas_call x1, Pallas kernels, body(): pl.pallas_call(functools.partial(open_kernel, rows, reps), out_shape=(sha...  25.7 us
    unnamed x18, local copies, waits for them, and re-layouts  8.62 us
    pallas_call x1, Pallas kernels, body(): pl.pallas_call(functools.partial(front_kernel, rows, reps, blocks, tile),...  6.79 us
    pallas_call x1, Pallas kernels, body(): pl.pallas_call(back_kernel, out_shape=(shape((local, half), BF16), shape(...  4.43 us

profile of v1, /device:TPU:0, one launch (start us, length us, event | category | flops | bytes accessed | tf_op | source)
XLA Modules:
  0.0 124.6 jit_solution(2290494674887786131)
XLA Ops:
  0.6 0.7 pad.4.cols
  1.3 0.7 copy.18
  2.1 0.1 reduce
  2.2 0.1 convert_reduce_fusion
  2.4 0.1 copy.19.row_ids
  2.5 0.0 copy-start.4
  2.5 1.0 copy-done.4
  3.6 0.0 copy-start.5
  3.6 0.9 copy-done.5
  4.5 0.0 copy-start.6
  4.5 0.9 copy-done.6
  5.4 25.7 %shard_map.94 = (bf16[7,512,128]{2,1,0:T(8,128)(2,1)S(1)}, bf16[2,256,512]{2,1,0:T(8,128)(2,1)S(1)}, bf16[2,4,4,128,128]{4,3,2,1,0:T(8,128)(2,1)S(1)}, s32[2,8,128]{2,1,0:T(8,128)S(1)}) custom-call(bf16[512,128]{1,0:T(8,128)(2,1)S(1)} %copy-done.6, bf16[256,512]{1,0:T(8,128)(2,1)S(1)} %copy-done.5, bf16[4,4,128,128]{3,2,1,0:T(8,128)(2,1)S(1)} %copy-done.4, ...), custom_call_target="tpu_custom_call" | custom-call | tf_op jit(solution)/shard_map/pallas_call | solution.py:238
  31.1 0.0 copy-start
  31.1 1.0 copy-done
  32.1 0.0 copy-start.7
  32.1 0.9 copy-done.7
  33.0 6.8 %shard_map.95 = (bf16[512,3584]{1,0:T(8,128)(2,1)}, bf16[512,128]{1,0:T(8,128)(2,1)S(1)}, f32[512,256]{1,0:T(8,128)S(1)}, bf16[512,256]{1,0:T(8,128)(2,1)S(1)}, ...) custom-call(bf16[2,4,4,128,128]{4,3,2,1,0:T(8,128)(2,1)S(1)} %get-tuple-, ...), custom_call_target="tpu_custom_call" | custom-call | tf_op jit(solution)/shard_map/pallas_call | solution.py:251
  39.8 0.0 copy-start.2
  39.8 1.5 %copy-done.2 = bf16[7,256,512]{2,1,0:T(8,128)(2,1)S(1)} copy-done((bf16[7,256,512]{2,1,0:T(8,128)(2,1)S(1)}, bf16[7,256,512]{2,1,0:T(8,128)(2,1)}, u32[]{:S(2)}) %copy-start.2) | copy-done | bytes 1835032
  41.3 45.3 %shard_map.96 = (bf16[7,512,256]{2,1,0:T(8,128)(2,1)S(1)}, bf16[6,256,512]{2,1,0:T(8,128)(2,1)S(1)}) custom-call(bf16[512,256]{1,0:T(8,128)(2,1)S(1)} %get-tuple-element.25.hidden, bf16[7,256,512]{2,1,0:T(8,128)(2,1)S(1)} %copy-done.2), custom_call_target="tpu_custom_call" | custom-call | tf_op jit(solution)/shard_map/pallas_call | solution.py:267
  86.6 0.0 copy-start.3
  86.6 1.2 copy-done.3
  87.9 0.0 copy-start.1
  87.9 4.4 %shard_map.97 = (bf16[512,256]{1,0:T(8,128)(2,1)S(1)}, f32[640,256]{1,0:T(8,128)S(1)}) custom-call(bf16[512,3584]{1,0:T(8,128)(2,1)} %get-tuple-element.24.dense, bf16[7,512,256]{2,1,0:T(8,128)(2,1)} %copy-done.3, bf16[6,256,512]{2,1,0:T(8,128)(2,1)S(1)} %get-tuple-element.28.term_band, bf16[512,128]{1,0:T(8,128)(2,1)S(1)} %get-tuple-element.29.first, ...), custom_call_target="tpu_custom_call" | custom-call | tf_op jit(solution)/shard_map/pallas_call | solution.py:276
  92.3 28.4 %shard_map.98 = (bf16[2,256,256]{2,1,0:T(8,128)(2,1)S(1)}, f32[2,2,8,40,256]{4,3,2,1,0:T(8,128)S(1)}) custom-call(bf16[2,256,256]{2,1,0:T(8,128)(2,1)S(1)} %bitcast.22, f32[2,8,40,256]{3,2,1,0:T(8,128)S(1)} %bitcast.21), custom_call_target="tpu_custom_call" | custom-call | tf_op jit(solution)/shard_map/pallas_call | solution.py:287
  120.7 0.1 copy.20
  120.8 0.0 copy-done.1
  120.9 1.0 convolution_convert_fusion
  121.9 0.1 slice.14
  122.0 0.8 copy.22
  122.8 1.0 copy.24
  123.8 0.7 copy.23
  (4 shorter events, 0.1 us)
Async XLA Ops:
  2.5 1.0 copy-start.4
  3.6 0.9 copy-start.5
  4.5 0.9 copy-start.6
  31.1 1.0 copy-start
  32.1 0.9 copy-start.7
  39.8 1.5 %copy-start.2 = (bf16[7,256,512]{2,1,0:T(8,128)(2,1)S(1)}, bf16[7,256,512]{2,1,0:T(8,128)(2,1)}, u32[]{:S(2)}) copy-start(bf16[7,256,512]{2,1,0:T(8,128)(2,1)} %get-tuple-element.26.terms) | copy-start | bytes 5505028
  86.6 1.2 copy-start.3
  87.9 33.0 %copy-start.1 = (bf16[512,512]{1,0:T(8,128)(2,1)S(1)}, bf16[512,512]{1,0:T(8,128)(2,1)}, u32[]{:S(2)}) copy-start(bf16[512,512]{1,0:T(8,128)(2,1)} %w2.1) | copy-start | bytes 1572868

commit v2 on v1

--- a/solution.py
+++ b/solution.py
@@ -9,9 +9,9 @@
 
 HOPS = 3
 SPAN = 2 * HOPS + 1
-SHIFTS = [s for s in range(-HOPS, HOPS + 1) if s]
 MESH = pl.DeviceIdType.MESH
 ANY = pl.BlockSpec(memory_space=pl.ANY)
+HBM = pl.BlockSpec(memory_space=pltpu.HBM)
 VMEM = pl.BlockSpec(memory_space=pltpu.VMEM)
 SMEM = pl.BlockSpec(memory_space=pltpu.SMEM)
 F32 = jnp.float32
@@ -36,31 +36,66 @@
     )
 
 
+def places(rows):
+    row, rep = lax.axis_index("row"), lax.axis_index("rep")
+    core = lax.rem(row, 2)
+    flip, far = 1 - 2 * core, 6 * core - 3
+
+    def at(shift):
+        return (lax.rem(row + shift + rows, rows), rep)
+
+    return flip, far, at
+
+
+def start_rows(rows, src, band, send, recv, base):
+    flip, far, at = places(rows)
+    copies = [remote(src, band.at[HOPS - shift], send, recv, base + n, at(shift))
+              for n, shift in enumerate((2, -2, far, flip))]
+    for copy in copies:
+        copy.start()
+    return copies
+
+
+def finish_rows(rows, copies, band, send, recv, base):
+    flip, far, at = places(rows)
+    passed = []
+    for n, shift in enumerate((2, -2)):
+        copies[n].wait_recv()
+        step = remote(band.at[HOPS - shift], band.at[HOPS - shift - flip], send, recv, base + n, at(flip))
+        step.start()
+        passed.append(step)
+    for copy in copies[2:]:
+        copy.wait_recv()
+    for copy in copies:
+        copy.wait_send()
+    for copy in passed:
+        copy.wait()
+
+
 def open_kernel(rows, reps, feats, cot, tiles, cols, band, cots, all_tiles, all_cols, send, recv, local):
     row, rep = lax.axis_index("row"), lax.axis_index("rep")
-    near = [(lax.rem(row + s + rows, rows), rep) for s in SHIFTS]
+    flip, far, at = places(rows)
     others = [(row, lax.rem(rep + t, reps)) for t in range(1, reps)]
-    greet(near + others)
+    greet([at(2), at(-2), at(far), at(flip)] + others)
     copies, n = [], 0
     pieces = ((tiles, all_tiles), (cols, all_cols), (cot, cots))
     for peer in others:
         for src, dst in pieces:
             copies.append(remote(src, dst.at[rep], send, recv, n, peer))
             n += 1
-    for s, peer in zip(SHIFTS, near):
-        copies.append(remote(feats, band.at[HOPS - s], send, recv, n, peer))
-        n += 1
     for i, (src, dst) in enumerate(pieces):
         copies.append(pltpu.make_async_copy(src, dst.at[rep], local.at[i]))
     copies.append(pltpu.make_async_copy(feats, band.at[HOPS], local.at[3]))
     for copy in copies:
         copy.start()
-    for copy in copies:
-        copy.wait()
-
-
-def front_kernel(rows, reps, blocks, tile, tiles, cols, row_ids, band_ids, band, cots, w1, w2,
-                 dense, first_o, preact_o, hidden_o, scaled_o, terms_o, own_o, deg_o):
+    moved = start_rows(rows, feats, band, send, recv, n)
+    finish_rows(rows, moved, band, send, recv, n + 4)
+    for copy in copies:
+        copy.wait()
+
+
+def front_kernel(rows, reps, blocks, tile, tiles, cols, row_ids, band_ids, band, cots, w2,
+                 dense, first_o, terms_o, own_o, deg_o):
     row, rep = lax.axis_index("row"), lax.axis_index("rep")
     total = rows * blocks
     per = tiles.shape[2]
@@ -83,11 +118,8 @@
     summed = dot(dense[...], flat, (1, 0))
     first = ((summed + band[HOPS].astype(F32)) / degree).astype(BF16)
     first_o[...] = first
-    half = w1.shape[1] // reps
+    half = w2.shape[0] // reps
     at = pl.ds(pl.multiple_of(rep * half, half), half)
-    preact = dot(first, w1[:, at], (1, 0))
-    preact_o[...] = preact
-    hidden_o[...] = jnp.maximum(preact, 0.0).astype(BF16)
     pulled = dot(cots[...].reshape(local, -1), w2[at, :], (1, 1))
     scaled = (pulled / degree).astype(BF16)
     scaled_t = scaled.astype(F32).T.astype(BF16)
@@ -96,41 +128,58 @@
         if s == HOPS:
             own_o[...] = part.T + scaled.astype(F32)
         terms_o[s] = part.astype(BF16)
-    scaled_o[...] = scaled
-
-
-def band_kernel(rows, hidden, terms, hid_band, term_band, send, recv, local):
-    row, rep = lax.axis_index("row"), lax.axis_index("rep")
-    near = [(lax.rem(row + s + rows, rows), rep) for s in SHIFTS]
-    greet(near)
-    copies, n = [], 0
-    for s, peer in zip(SHIFTS, near):
-        copies.append(remote(hidden, hid_band.at[HOPS - s], send, recv, n, peer))
-        where = (HOPS - s) if s > 0 else (HOPS - s - 1)
-        copies.append(remote(terms.at[HOPS + s], term_band.at[where], send, recv, n + 1, peer))
-        n += 2
-    copies.append(pltpu.make_async_copy(hidden, hid_band.at[HOPS], local.at[0]))
-    for copy in copies:
-        copy.start()
-    for copy in copies:
-        copy.wait()
-
-
-def back_kernel(dense, hid_band, term_band, first, preact, own, deg, cots, second_o, grads_o):
-    local, half = preact.shape
-    summed = dot(dense[...], hid_band[...].reshape(SPAN * local, half), (1, 0))
-    second = ((summed + hid_band[HOPS].astype(F32)) / deg[...]).astype(BF16)
+
+
+def band_kernel(rows, first, terms, first_band, term_band, pair, joint, send, recv, local):
+    flip, far, at = places(rows)
+    greet([at(2), at(-2), at(far), at(flip)])
+    joined = [remote(terms.at[HOPS + shift + flip], pair.at[n], send, recv, n, at(flip))
+              for n, shift in enumerate((2, -2))]
+    for copy in joined:
+        copy.start()
+    direct = [remote(terms.at[HOPS + far], term_band.at[2], send, recv, 2, at(far))]
+    direct[0].start()
+    moved = start_rows(rows, first, first_band, send, recv, 3)
+    keep = pltpu.make_async_copy(first, first_band.at[HOPS], local.at[0])
+    keep.start()
+    direct.append(remote(terms.at[HOPS + flip], term_band.at[3], send, recv, 7, at(flip)))
+    direct[1].start()
+    for n, shift in enumerate((2, -2)):
+        joined[n].wait_recv()
+        joint[n] = (terms[HOPS + shift].astype(F32) + pair[n].astype(F32)).astype(BF16)
+        step = remote(joint.at[n], term_band.at[n], send, recv, 8 + n, at(shift))
+        step.start()
+        direct.append(step)
+    finish_rows(rows, moved, first_band, send, recv, 10)
+    keep.wait()
+    for copy in joined:
+        copy.wait_send()
+    for copy in direct:
+        copy.wait()
+
+
+def back_kernel(reps, dense, first_band, term_band, w1, own, deg, cots, second_o, grads_o):
+    rep = lax.axis_index("rep")
+    local, half = own.shape
+    weight = w1[:, pl.ds(pl.multiple_of(rep * half, half), half)]
+    preact = dot(first_band[HOPS], weight, (1, 0))
+    mine = jnp.maximum(preact, 0.0).astype(BF16)
+    summed = mine.astype(F32)
+    for s in range(SPAN):
+        hidden = mine if s == HOPS else jnp.maximum(dot(first_band[s], weight, (1, 0)), 0.0).astype(BF16)
+        summed = summed + dot(dense[:, s * local:(s + 1) * local], hidden, (1, 0))
+    second = (summed / deg[...]).astype(BF16)
     second_o[...] = second
     out = dot(second, cots[...].reshape(local, -1), (0, 0))
     width = out.shape[1] // half
     for i in range(width):
         grads_o[i * half:(i + 1) * half, :] = out[:, i * half:(i + 1) * half]
     got = term_band[0].astype(F32)
-    for i in range(1, SPAN - 1):
+    for i in range(1, 4):
         got = got + term_band[i].astype(F32)
     back = got.T + own[...]
-    delta = jnp.where(preact[...] > 0.0, back, 0.0).astype(BF16)
-    grads_o[width * half:, :] = dot(first[...], delta, (0, 0))
+    delta = jnp.where(preact > 0.0, back, 0.0).astype(BF16)
+    grads_o[width * half:, :] = dot(first_band[HOPS], delta, (0, 0))
 
 
 def swap_kernel(reps, second, full, send, recv, local):
@@ -170,7 +219,7 @@
     for t, copy in enumerate(copies):
         copy.wait_recv()
         total = total + parts[t]
-    whole[rep, core, chip] = total
+    whole[rep, core, chip] = total.astype(BF16)
     base = base + chips - 1
     spread = [remote(whole.at[rep, core, chip], whole.at[rep, core, chip], send, recv, base + t, peer)
               for t, peer in enumerate(peers)]
@@ -243,50 +292,47 @@
             shape((reps,) + adjacency_tiles.shape, BF16),
             shape((reps, 8, 128), jnp.int32),
         ),
-        in_specs=[ANY] * 4,
+        in_specs=[HBM] * 4,
         out_specs=(ANY,) * 4,
-        scratch_shapes=sems(3 * (reps - 1) + 2 * HOPS),
+        scratch_shapes=sems(3 * (reps - 1) + 6),
         compiler_params=params(0),
     )(features, cotangent, adjacency_tiles, padded)
-    dense, first, preact, hidden, scaled, terms, own, degree = pl.pallas_call(
+    dense, first, terms, own, degree = pl.pallas_call(
         functools.partial(front_kernel, rows, reps, blocks, tile),
         out_shape=(
             shape((local, SPAN * local), BF16),
             shape((local, fin), BF16),
-            shape((local, half), F32),
-            shape((local, half), BF16),
-            shape((local, half), BF16),
             shape((SPAN, half, local), BF16),
             shape((local, half), F32),
             shape((local, 1), F32),
         ),
-        in_specs=[VMEM, SMEM] + [VMEM] * 6,
-        out_specs=(VMEM,) * 8,
+        in_specs=[VMEM, SMEM] + [VMEM] * 5,
+        out_specs=(VMEM,) * 5,
         compiler_params=params(),
-    )(all_tiles, all_cols, row_ids, band_ids, band, cots, input_weight, output_weight)
-    hid_band, term_band = pl.pallas_call(
+    )(all_tiles, all_cols, row_ids, band_ids, band, cots, output_weight)
+    first_band, term_band = pl.pallas_call(
         functools.partial(band_kernel, rows),
-        out_shape=(shape((SPAN, local, half), BF16), shape((SPAN - 1, half, local), BF16)),
-        in_specs=[ANY] * 2,
-        out_specs=(ANY,) * 2,
-        scratch_shapes=sems(4 * HOPS),
+        out_shape=(shape((SPAN, local, fin), BF16), shape((4, half, local), BF16)),
+        in_specs=[VMEM] * 2,
+        out_specs=(VMEM,) * 2,
+        scratch_shapes=[pltpu.VMEM((2, half, local), BF16)] * 2 + sems(12),
         compiler_params=params(1),
-    )(hidden, terms)
+    )(first, terms)
     tall = hid * hid // reps // half + fin
     second, grads = pl.pallas_call(
-        back_kernel,
+        functools.partial(back_kernel, reps),
         out_shape=(shape((local, half), BF16), shape((tall, half), F32)),
-        in_specs=[VMEM] * 8,
+        in_specs=[VMEM] * 7,
         out_specs=(VMEM,) * 2,
         compiler_params=params(),
-    )(dense, hid_band, term_band, first, preact, own, degree, cots)
+    )(dense, first_band, term_band, input_weight, own, degree, cots)
     second = second.reshape(reps, quarter, half)
     if rows <= 16 and rows % 2 == 0 and tall % (8 * rows) == 0:
         chips = rows // 2
         chunk = tall // rows
         full, whole = pl.pallas_call(
             functools.partial(sum_kernel, chips, reps),
-            out_shape=(shape((reps, quarter, half), BF16), shape((reps, 2, chips, chunk, half), F32)),
+            out_shape=(shape((reps, quarter, half), BF16), shape((reps, 2, chips, chunk, half), BF16)),
             in_specs=[ANY, VMEM],
             out_specs=(ANY, VMEM),
             scratch_shapes=[
@@ -308,6 +354,7 @@
         )(second)
         whole = lax.all_gather(lax.psum(grads, "row"), "rep", axis=0)
     scores = dot(full.transpose(1, 0, 2).reshape(quarter, hid), output_weight, (1, 0)).astype(BF16)
+    whole = whole.astype(F32)
     grad_input = whole[:, tall - fin:].transpose(1, 0, 2).reshape(fin, hid)
     grad_output = whole[:, :tall - fin].reshape(reps, hid // half, half, half)
     grad_output = grad_output.transpose(0, 2, 1, 3).reshape(hid, hid)

time: 127 us -> 88.7 us (0.70); the launches traced: 125 us -> 88.4 us
  Pallas kernels: 111 us -> 78.8 us
  local copies, waits for them, and re-layouts: 11.9 us -> 7.33 us
    pallas_call x1, Pallas kernels: 45.3 us -> 21.5 us  [body(): pl.pallas_call(functools.partial(band_kernel, rows), out_shape=(shape((SP...]
    pallas_call x1, Pallas kernels: 28.4 us -> 23.5 us  [body(): pl.pallas_call(functools.partial(sum_kernel, chips, reps), out_shape=(sha...]
    unnamed x18 -> x12, local copies, waits for them, and re-layouts: 8.62 us -> 3.96 us
    pallas_call x1, Pallas kernels: 6.79 us -> 3.82 us  [body(): pl.pallas_call(functools.partial(front_kernel, rows, reps, blocks, tile),...]
where the time goes in v2:
time: 88.7 us; the launch traced here: 88.4 us
  Pallas kernels  78.8 us (89%)
  local copies, waits for them, and re-layouts  7.33 us (8%)
  matrix products  1.03 us (1%)
    pallas_call x1, Pallas kernels, body(): pl.pallas_call(functools.partial(open_kernel, rows, reps), out_shape=(sha...  25 us
    pallas_call x1, Pallas kernels, body(): pl.pallas_call(functools.partial(sum_kernel, chips, reps), out_shape=(sha...  23.5 us
    pallas_call x1, Pallas kernels, body(): pl.pallas_call(functools.partial(band_kernel, rows), out_shape=(shape((SP...  21.5 us
    pallas_call x1, Pallas kernels, body(): pl.pallas_call(functools.partial(back_kernel, reps), out_shape=(shape((lo...  4.98 us
    unnamed x12, local copies, waits for them, and re-layouts  3.96 us
    pallas_call x1, Pallas kernels, body(): pl.pallas_call(functools.partial(front_kernel, rows, reps, blocks, tile),...  3.82 us

profile of v2, /device:TPU:0, one launch (start us, length us, event | category | flops | bytes accessed | tf_op | source)
XLA Modules:
  0.0 88.4 jit_solution(6438598696266059050)
XLA Ops:
  0.6 0.0 copy-start
  0.6 0.7 pad.4.cols
  1.4 0.7 copy.18
  2.2 0.1 reduce
  2.3 0.1 convert_reduce_fusion
  2.4 0.1 copy.19.row_ids
  2.6 0.0 copy-start.1
  2.6 1.0 %copy-done.1 = bf16[4,4,128,128]{3,2,1,0:T(8,128)(2,1)S(1)} copy-done((bf16[4,4,128,128]{3,2,1,0:T(8,128)(2,1)S(1)}, bf16[4,4,128,128]{3,2,1,0:T(8,128)(2,1)}, u32[]{:S(2)}) %copy-start.1) | copy-done | bytes 524312
  3.6 0.0 copy-start.2
  3.6 0.9 %copy-done.2 = bf16[256,512]{1,0:T(8,128)(2,1)S(1)} copy-done((bf16[256,512]{1,0:T(8,128)(2,1)S(1)}, bf16[256,512]{1,0:T(8,128)(2,1)}, u32[]{:S(2)}) %copy-start.2) | copy-done | bytes 262168
  4.6 0.0 copy-start.4
  4.6 0.9 %copy-done.4 = bf16[512,128]{1,0:T(8,128)(2,1)S(1)} copy-done((bf16[512,128]{1,0:T(8,128)(2,1)S(1)}, bf16[512,128]{1,0:T(8,128)(2,1)}, u32[]{:S(2)}) %copy-start.4) | copy-done | bytes 131096
  5.5 25.0 %shard_map.94 = (bf16[7,512,128]{2,1,0:T(8,128)(2,1)S(1)}, bf16[2,256,512]{2,1,0:T(8,128)(2,1)S(1)}, bf16[2,4,4,128,128]{4,3,2,1,0:T(8,128)(2,1)S(1)}, s32[2,8,128]{2,1,0:T(8,128)S(1)}) custom-call(bf16[512,128]{1,0:T(8,128)(2,1)S(1)} %copy-done.4, bf16[256,512]{1,0:T(8,128)(2,1)S(1)} %copy-done.2, bf16[4,4,128,128]{3,2,1,0:T(8,128)(2,1)S(1)} %copy-done.1, ...), custom_call_target="tpu_custom_call" | custom-call | tf_op jit(solution)/shard_map/pallas_call | solution.py:287
  30.5 0.0 copy-done
  30.5 3.8 %shard_map.95 = (bf16[512,3584]{1,0:T(8,128)(2,1)}, bf16[512,128]{1,0:T(8,128)(2,1)S(1)}, bf16[7,256,512]{2,1,0:T(8,128)(2,1)S(1)}, f32[512,256]{1,0:T(8,128)S(1)}, f32[512,1]{1,0:T(8,128)S(1)}) custom-call(bf16[2,4,4,128,128]{4,3,2,1,0:T(8,128)(2,1)S(1)} %get-tuple-element.18.tiles, s32[2,8,128]{2,1,0:T(8,128)S(1)} %get-tuple-element.19.cols, ...), custom_call_target="tpu_custom_call" | custom-call | tf_op jit(solution)/shard_map/pallas_call | solution.py:300
  34.4 0.0 copy-start.3
  34.4 21.5 %shard_map.96 = (bf16[7,512,128]{2,1,0:T(8,128)(2,1)S(1)}, bf16[4,256,512]{2,1,0:T(8,128)(2,1)S(1)}) custom-call(bf16[512,128]{1,0:T(8,128)(2,1)S(1)} %get-tuple-element.23.first, bf16[7,256,512]{2,1,0:T(8,128)(2,1)S(1)} %get-tuple-element.24.terms), custom_call_target="tpu_custom_call" | custom-call | tf_op jit(solution)/shard_map/pallas_call | solution.py:313
  55.9 0.0 copy-done.3
  55.9 5.0 %shard_map.97 = (bf16[512,256]{1,0:T(8,128)(2,1)S(1)}, f32[640,256]{1,0:T(8,128)S(1)}) custom-call(bf16[512,3584]{1,0:T(8,128)(2,1)} %get-tuple-element.22.dense, bf16[7,512,128]{2,1,0:T(8,128)(2,1)S(1)} %get-tuple-element.25.first_band, bf16[4,256,512]{2,1,0:T(8,128)(2,1)S(1)} %get-tuple-element.26.term_band, bf16[128,512]{1,0:T(8,128)(2,1)S(1)} %copy-done.3, ...), custom_call_target="tpu_custom_call" | custom-call | tf_op jit(solution)/shard_map/pallas_call | solution.py:322
  60.8 23.5 %shard_map.98 = (bf16[2,256,256]{2,1,0:T(8,128)(2,1)S(1)}, bf16[2,2,8,40,256]{4,3,2,1,0:T(8,128)(2,1)S(1)}) custom-call(bf16[2,256,256]{2,1,0:T(8,128)(2,1)S(1)} %bitcast.22, f32[2,8,40,256]{3,2,1,0:T(8,128)S(1)} %bitcast.21), custom_call_target="tpu_custom_call" | custom-call | tf_op jit(solution)/shard_map/pallas_call | solution.py:333
  84.4 0.1 copy.20
  84.5 1.0 %convolution_convert_fusion = bf16[256,512]{1,0:T(8,128)(2,1)} fusion(bf16[256,512]{0,1:T(8,128)(2,1)S(1)} %bitcast.28, bf16[512,512]{1,0:T(8,128)(2,1)S(1)} %copy-done), kind=kOutput, calls=%fused_computation | convolution fusion | flops 134348800 | bytes 1048576 | tf_op jit(solution)/shard_map/dot_general | solution.py:22
  85.5 0.1 bitcast_convert_fusion
  85.7 0.1 slice.14
  85.8 0.8 copy.22
  86.6 1.0 %copy.24 = f32[64,8,2,256]{3,1,2,0:T(8,128)} copy(f32[64,8,2,256]{3,2,1,0:T(2,128)S(1)} %bitcast.26) | data formatting | bytes 2097152
  87.6 0.7 copy.23
  (4 shorter events, 0.1 us)
Async XLA Ops:
  0.6 29.9 %copy-start = (bf16[512,512]{1,0:T(8,128)(2,1)S(1)}, bf16[512,512]{1,0:T(8,128)(2,1)}, u32[]{:S(2)}) copy-start(bf16[512,512]{1,0:T(8,128)(2,1)} %w2.1) | copy-start | bytes 1572868
  2.6 1.0 %copy-start.1 = (bf16[4,4,128,128]{3,2,1,0:T(8,128)(2,1)S(1)}, bf16[4,4,128,128]{3,2,1,0:T(8,128)(2,1)}, u32[]{:S(2)}) copy-start(bf16[4,4,128,128]{3,2,1,0:T(8,128)(2,1)} %tiles.1) | copy-start | bytes 1572868
  3.6 0.9 %copy-start.2 = (bf16[256,512]{1,0:T(8,128)(2,1)S(1)}, bf16[256,512]{1,0:T(8,128)(2,1)}, u32[]{:S(2)}) copy-start(bf16[256,512]{1,0:T(8,128)(2,1)} %cot.1) | copy-start | bytes 786436
  4.6 0.9 %copy-start.4 = (bf16[512,128]{1,0:T(8,128)(2,1)S(1)}, bf16[512,128]{1,0:T(8,128)(2,1)}, u32[]{:S(2)}) copy-start(bf16[512,128]{1,0:T(8,128)(2,1)} %feats.1) | copy-start | bytes 393220
  34.4 21.5 %copy-start.3 = (bf16[128,512]{1,0:T(8,128)(2,1)S(1)}, bf16[128,512]{1,0:T(8,128)(2,1)}, u32[]{:S(2)}) copy-start(bf16[128,512]{1,0:T(8,128)(2,1)} %w1.1) | copy-start | bytes 393220

commit v3 on v2

--- a/solution.py
+++ b/solution.py
@@ -194,42 +194,107 @@
         copy.wait()
 
 
-def sum_kernel(chips, reps, second, grads, full, whole, mine, pair, parts, send, recv, local):
+def rest_kernel(rows, reps, first, terms, dense, w1, own, deg, cots, full, whole,
+                first_band, term_band, pair, joint, second_s, go, gi, go_pair, gi_pair, go_mine, gi_mine,
+                go_parts, gi_parts, send, recv, local):
     row, rep = lax.axis_index("row"), lax.axis_index("rep")
+    flip, far, at = places(rows)
+    chips = rows // 2
     chip, core = row // 2, lax.rem(row, 2)
-    sibling = (chip * 2 + 1 - core, rep)
+    sibling = at(flip)
     turns = [lax.rem(chip + t, chips) for t in range(1, chips)]
     peers = [(q * 2 + core, rep) for q in turns]
     others = [(row, lax.rem(rep + t, reps)) for t in range(1, reps)]
-    greet([sibling] + peers + others)
-    a = remote(grads.at[1 - core], pair, send, recv, 0, sibling)
-    a.start()
-    early = [remote(second.at[peer[1]], full.at[rep], send, recv, 1 + n, peer) for n, peer in enumerate(others)]
-    early.append(pltpu.make_async_copy(second.at[rep], full.at[rep], local.at[0]))
-    for copy in early:
-        copy.start()
-    base = reps
-    a.wait()
-    mine[...] = grads[core] + pair[...]
-    copies = [remote(mine.at[q], parts.at[t], send, recv, base + t, peer)
-              for t, (q, peer) in enumerate(zip(turns, peers))]
-    for copy in copies:
-        copy.start()
-    total = mine[chip]
-    for t, copy in enumerate(copies):
-        copy.wait_recv()
-        total = total + parts[t]
-    whole[rep, core, chip] = total.astype(BF16)
+    greet([sibling, at(far)] + peers + others)
+    joined = [remote(terms.at[HOPS + shift + flip], pair.at[n], send, recv, n, sibling)
+              for n, shift in enumerate((2, -2))]
+    for copy in joined:
+        copy.start()
+    moved = start_rows(rows, first, first_band, send, recv, 3)
+    direct = [remote(terms.at[HOPS + far], term_band.at[2], send, recv, 2, at(far))]
+    direct[0].start()
+    keep = pltpu.make_async_copy(first, first_band.at[HOPS], local.at[0])
+    keep.start()
+    direct.append(remote(terms.at[HOPS + flip], term_band.at[3], send, recv, 7, sibling))
+    direct[1].start()
+    for n, shift in enumerate((2, -2)):
+        joined[n].wait_recv()
+        joint[n] = (terms[HOPS + shift].astype(F32) + pair[n].astype(F32)).astype(BF16)
+        step = remote(joint.at[n], term_band.at[n], send, recv, 8 + n, at(shift))
+        step.start()
+        direct.append(step)
+    finish_rows(rows, moved, first_band, send, recv, 10)
+    keep.wait()
+
+    size, half = own.shape
+    weight = w1[:, pl.ds(pl.multiple_of(rep * half, half), half)]
+    mine_first = first_band[HOPS]
+    preact = dot(mine_first, weight, (1, 0))
+    mine = jnp.maximum(preact, 0.0).astype(BF16)
+    summed = mine.astype(F32)
+    for s in range(SPAN):
+        hidden = mine if s == HOPS else jnp.maximum(dot(first_band[s], weight, (1, 0)), 0.0).astype(BF16)
+        summed = summed + dot(dense[:, s * size:(s + 1) * size], hidden, (1, 0))
+    second = (summed / deg[...]).astype(BF16)
+    second_s[...] = second.reshape(second_s.shape)
+    base = 12
+    late = [remote(second_s.at[peer[1]], full.at[rep], send, recv, base + n, peer) for n, peer in enumerate(others)]
+    late.append(pltpu.make_async_copy(second_s.at[rep], full.at[rep], local.at[1]))
+    for copy in late:
+        copy.start()
+    base = base + reps - 1
+    out = dot(second, cots[...].reshape(size, -1), (0, 0))
+    width = out.shape[1] // half
+    out = jnp.concatenate([out[:, i * half:(i + 1) * half] for i in range(width)], axis=0)
+    go[...] = out.reshape(go.shape)
+
+    def fold(grads, got, total, parts, base):
+        a = remote(grads.at[1 - core], got, send, recv, base, sibling)
+        a.start()
+
+        def rest():
+            a.wait()
+            total[...] = grads[core] + got[...]
+            copies = [remote(total.at[q], parts.at[t], send, recv, base + 1 + t, peer)
+                      for t, (q, peer) in enumerate(zip(turns, peers))]
+            for copy in copies:
+                copy.start()
+            return copies
+
+        return rest
+
+    def gathered(copies, total, parts):
+        value = total[chip]
+        for t, copy in enumerate(copies):
+            copy.wait_recv()
+            value = value + parts[t]
+        return value
+
+    go_copies = fold(go, go_pair, go_mine, go_parts, base)()
+    base = base + chips
+    for copy in direct:
+        copy.wait()
+    got = term_band[0].astype(F32)
+    for i in range(1, 4):
+        got = got + term_band[i].astype(F32)
+    back = got.T + own[...]
+    delta = jnp.where(preact > 0.0, back, 0.0).astype(BF16)
+    gi[...] = dot(mine_first, delta, (0, 0)).reshape(gi.shape)
+    rest = fold(gi, gi_pair, gi_mine, gi_parts, base)
+    base = base + chips
+    go_total = gathered(go_copies, go_mine, go_parts)
+    gi_copies = rest()
+    gi_total = gathered(gi_copies, gi_mine, gi_parts)
+    whole[rep, core, chip] = jnp.concatenate([go_total, gi_total], axis=0).astype(BF16)
+    spot = whole.at[rep, core, chip]
+    spread = [remote(spot, spot, send, recv, base + t, peer) for t, peer in enumerate(peers)]
+    for copy in spread:
+        copy.start()
     base = base + chips - 1
-    spread = [remote(whole.at[rep, core, chip], whole.at[rep, core, chip], send, recv, base + t, peer)
-              for t, peer in enumerate(peers)]
-    for copy in spread:
-        copy.start()
-    for copy in copies:
+    for copy in joined + go_copies + gi_copies:
         copy.wait_send()
     for copy in spread:
         copy.wait()
-    base = base + chips - 1
     block = whole.at[rep, core]
     last = [remote(block, block, send, recv, base + n, peer) for n, peer in enumerate(others)]
     base = base + reps - 1
@@ -244,8 +309,22 @@
         side.append(step)
     for copy in last:
         copy.wait_send()
-    for copy in side + early:
-        copy.wait()
+    for copy in side + late:
+        copy.wait()
+
+
+def close_kernel(deep, full, whole, w2, scores_o, gi_o, go_o):
+    reps, half = full.shape[0], full.shape[2]
+    for j in range(reps):
+        at = slice(j * half, (j + 1) * half)
+        part = dot(full[j], w2[at, :], (1, 0))
+        total = part if j == 0 else total + part
+        part = whole[j].astype(F32)
+        gi_o[:, at] = part[..., deep:, :].reshape(gi_o.shape[0], half)
+        part = part[..., :deep, :].reshape(-1, half)
+        for i in range(part.shape[0] // half):
+            go_o[at, i * half:(i + 1) * half] = part[i * half:(i + 1) * half]
+    scores_o[...] = total.astype(BF16)
 
 
 def params(number=None):
@@ -293,7 +372,7 @@
             shape((reps, 8, 128), jnp.int32),
         ),
         in_specs=[HBM] * 4,
-        out_specs=(ANY,) * 4,
+        out_specs=(VMEM,) * 3 + (ANY,),
         scratch_shapes=sems(3 * (reps - 1) + 6),
         compiler_params=params(0),
     )(features, cotangent, adjacency_tiles, padded)
@@ -310,6 +389,46 @@
         out_specs=(VMEM,) * 5,
         compiler_params=params(),
     )(all_tiles, all_cols, row_ids, band_ids, band, cots, output_weight)
+    tall = hid * hid // reps // half + fin
+    if 6 < rows <= 16 and rows % 2 == 0 and fin % (8 * rows) == 0:
+        chips, deep, thin = rows // 2, hid // rows, fin // rows
+
+        def bank(*dims):
+            return pltpu.VMEM(dims, F32)
+
+        full, whole = pl.pallas_call(
+            functools.partial(rest_kernel, rows, reps),
+            out_shape=(
+                shape((reps, quarter, half), BF16),
+                shape((reps, 2, chips, deep + thin, half), BF16),
+            ),
+            in_specs=[VMEM] * 7,
+            out_specs=(VMEM,) * 2,
+            scratch_shapes=[
+                pltpu.VMEM((SPAN, local, fin), BF16),
+                pltpu.VMEM((4, half, local), BF16),
+                pltpu.VMEM((2, half, local), BF16),
+                pltpu.VMEM((2, half, local), BF16),
+                pltpu.VMEM((reps, quarter, half), BF16),
+                bank(2, chips, deep, half),
+                bank(2, chips, thin, half),
+                bank(chips, deep, half),
+                bank(chips, thin, half),
+                bank(chips, deep, half),
+                bank(chips, thin, half),
+                bank(chips - 1, deep, half),
+                bank(chips - 1, thin, half),
+            ] + sems(12 + 3 * reps + 3 * chips),
+            compiler_params=params(1),
+        )(first, terms, dense, input_weight, own, degree, cots)
+        scores, grad_input, grad_output = pl.pallas_call(
+            functools.partial(close_kernel, deep),
+            out_shape=(shape((quarter, hid), BF16), shape((fin, hid), F32), shape((hid, hid), F32)),
+            in_specs=[VMEM] * 3,
+            out_specs=(VMEM,) * 3,
+            compiler_params=params(),
+        )(full, whole, output_weight)
+        return scores, grad_input, grad_output
     first_band, term_band = pl.pallas_call(
         functools.partial(band_kernel, rows),
         out_shape=(shape((SPAN, local, fin), BF16), shape((4, half, local), BF16)),
@@ -318,7 +437,6 @@
         scratch_shapes=[pltpu.VMEM((2, half, local), BF16)] * 2 + sems(12),
         compiler_params=params(1),
     )(first, terms)
-    tall = hid * hid // reps // half + fin
     second, grads = pl.pallas_call(
         functools.partial(back_kernel, reps),
         out_shape=(shape((local, half), BF16), shape((tall, half), F32)),
@@ -327,34 +445,16 @@
         compiler_params=params(),
     )(dense, first_band, term_band, input_weight, own, degree, cots)
     second = second.reshape(reps, quarter, half)
-    if rows <= 16 and rows % 2 == 0 and tall % (8 * rows) == 0:
-        chips = rows // 2
-        chunk = tall // rows
-        full, whole = pl.pallas_call(
-            functools.partial(sum_kernel, chips, reps),
-            out_shape=(shape((reps, quarter, half), BF16), shape((reps, 2, chips, chunk, half), BF16)),
-            in_specs=[ANY, VMEM],
-            out_specs=(ANY, VMEM),
-            scratch_shapes=[
-                pltpu.VMEM((chips, chunk, half), F32),
-                pltpu.VMEM((chips, chunk, half), F32),
-                pltpu.VMEM((chips - 1, chunk, half), F32),
-            ] + sems(3 * reps + 2 * chips),
-            compiler_params=params(2),
-        )(second, grads.reshape(2, chips, chunk, half))
-        whole = whole.reshape(reps, tall, half)
-    else:
-        full = pl.pallas_call(
-            functools.partial(swap_kernel, reps),
-            out_shape=shape((reps, quarter, half), BF16),
-            in_specs=[ANY],
-            out_specs=ANY,
-            scratch_shapes=sems(reps),
-            compiler_params=params(2),
-        )(second)
-        whole = lax.all_gather(lax.psum(grads, "row"), "rep", axis=0)
+    full = pl.pallas_call(
+        functools.partial(swap_kernel, reps),
+        out_shape=shape((reps, quarter, half), BF16),
+        in_specs=[ANY],
+        out_specs=ANY,
+        scratch_shapes=sems(reps),
+        compiler_params=params(2),
+    )(second)
+    whole = lax.all_gather(lax.psum(grads, "row"), "rep", axis=0)
     scores = dot(full.transpose(1, 0, 2).reshape(quarter, hid), output_weight, (1, 0)).astype(BF16)
-    whole = whole.astype(F32)
     grad_input = whole[:, tall - fin:].transpose(1, 0, 2).reshape(fin, hid)
     grad_output = whole[:, :tall - fin].reshape(reps, hid // half, half, half)
     grad_output = grad_output.transpose(0, 2, 1, 3).reshape(hid, hid)

time: 88.7 us -> 79.1 us (0.89)
  Pallas kernels: 78.8 us -> 72.3 us
  local copies, waits for them, and re-layouts: 7.33 us -> 5.54 us
  matrix products: 1.03 us -> 0 us
    pallas_call x3 -> x2, Pallas kernels: 50 us -> 43.4 us  [the longest x1 42 us: body(): pl.pallas_call(functools.partial(rest_kernel, rows, reps), out_shape=(sha...]
    reshape x2 -> x0, local copies, waits for them, and re-layouts: 1.54 us -> none  [the longest x1 0.81 us: body(): grad_output = whole[:, :tall - fin].reshape(reps, hid // half, half, half)]
    dot_general x1 -> x0, matrix products: 1.03 us -> none  [dot(): lax.dot_general(a, b, ((dims[:1], dims[1:]), ((), ())), preferred_element...]
where the time goes in v3:
time: 79.1 us; the launch traced here: 78.8 us
  Pallas kernels  72.3 us (91%)
  local copies, waits for them, and re-layouts  5.54 us (7%)
    pallas_call x1, Pallas kernels, body(): pl.pallas_call(functools.partial(rest_kernel, rows, reps), out_shape=(sha...  42 us
    pallas_call x1, Pallas kernels, body(): pl.pallas_call(functools.partial(open_kernel, rows, reps), out_shape=(sha...  25 us
    unnamed x12, local copies, waits for them, and re-layouts  3.94 us
    pallas_call x1, Pallas kernels, body(): pl.pallas_call(functools.partial(front_kernel, rows, reps, blocks, tile),...  3.8 us

profile of v3, /device:TPU:0, one launch (start us, length us, event | category | flops | bytes accessed | tf_op | source)
XLA Modules:
  0.0 78.8 jit_solution(8769764618618415167)
XLA Ops:
  0.6 0.0 copy-start.4
  0.6 0.7 pad.4.cols
  1.4 0.7 copy.13
  2.1 0.1 reduce
  2.3 0.1 convert_reduce_fusion
  2.4 0.1 copy.14.row_ids
  2.6 0.0 copy-start.2
  2.6 1.0 %copy-done.2 = bf16[4,4,128,128]{3,2,1,0:T(8,128)(2,1)S(1)} copy-done((bf16[4,4,128,128]{3,2,1,0:T(8,128)(2,1)S(1)}, bf16[4,4,128,128]{3,2,1,0:T(8,128)(2,1)}, u32[]{:S(2)}) %copy-start.2) | copy-done | bytes 524312
  3.6 0.0 copy-start.3
  3.6 0.9 %copy-done.3 = bf16[256,512]{1,0:T(8,128)(2,1)S(1)} copy-done((bf16[256,512]{1,0:T(8,128)(2,1)S(1)}, bf16[256,512]{1,0:T(8,128)(2,1)}, u32[]{:S(2)}) %copy-start.3) | copy-done | bytes 262168
  4.6 0.0 copy-start.5
  4.6 0.9 %copy-done.5 = bf16[512,128]{1,0:T(8,128)(2,1)S(1)} copy-done((bf16[512,128]{1,0:T(8,128)(2,1)S(1)}, bf16[512,128]{1,0:T(8,128)(2,1)}, u32[]{:S(2)}) %copy-start.5) | copy-done | bytes 131096
  5.5 25.0 %shard_map.94 = (bf16[7,512,128]{2,1,0:T(8,128)(2,1)S(1)}, bf16[2,256,512]{2,1,0:T(8,128)(2,1)S(1)}, bf16[2,4,4,128,128]{4,3,2,1,0:T(8,128)(2,1)S(1)}, s32[2,8,128]{2,1,0:T(8,128)S(1)}) custom-call(bf16[512,128]{1,0:T(8,128)(2,1)S(1)} %copy-done.5, bf16[256,512]{1,0:T(8,128)(2,1)S(1)} %copy-done.3, bf16[4,4,128,128]{3,2,1,0:T(8,128)(2,1)S(1)} %copy-done.2, ...), custom_call_target="tpu_custom_call" | custom-call | tf_op jit(solution)/shard_map/pallas_call | solution.py:366
  30.5 0.0 copy-start
  30.5 1.0 %copy-done = bf16[512,512]{1,0:T(8,128)(2,1)S(1)} copy-done((bf16[512,512]{1,0:T(8,128)(2,1)S(1)}, bf16[512,512]{1,0:T(8,128)(2,1)}, u32[]{:S(2)}) %copy-start) | copy-done | bytes 524312
  31.6 3.8 %shard_map.95 = (bf16[512,3584]{1,0:T(8,128)(2,1)}, bf16[512,128]{1,0:T(8,128)(2,1)S(1)}, bf16[7,256,512]{2,1,0:T(8,128)(2,1)S(1)}, f32[512,256]{1,0:T(8,128)S(1)}, f32[512,1]{1,0:T(8,128)S(1)}) custom-call(bf16[2,4,4,128,128]{4,3,2,1,0:T(8,128)(2,1)S(1)} %get-tuple-element.14.tiles, s32[2,8,128]{2,1,0:T(8,128)S(1)} %get-tuple-element.15.cols, ...), custom_call_target="tpu_custom_call" | custom-call | tf_op jit(solution)/shard_map/pallas_call | solution.py:379
  35.4 0.0 copy-start.1
  35.4 0.0 copy-done.4
  35.4 42.0 %shard_map.96 = (bf16[2,256,256]{2,1,0:T(8,128)(2,1)S(1)}, bf16[2,2,8,40,256]{4,3,2,1,0:T(8,128)(2,1)S(1)}) custom-call(bf16[512,128]{1,0:T(8,128)(2,1)S(1)} %get-tuple-element.18.first, bf16[7,256,512]{2,1,0:T(8,128)(2,1)S(1)} %get-tuple-element.19.terms, bf16[512,3584]{1,0:T(8,128)(2,1)} %get-tuple-element.20.dense, bf16[128,512]{1,0:T(8,128)(2,1)S(1)} %copy-done.4, ...), custom_call_target="tpu_custom_call" | custom-call | tf_op jit(solution)/shard_map/pallas_call | solution.py:399
  77.4 0.0 copy-done.1
  77.4 1.4 %shard_map.97 = (bf16[256,512]{1,0:T(8,128)(2,1)}, f32[128,512]{1,0:T(8,128)}, f32[512,512]{1,0:T(8,128)}) custom-call(bf16[2,256,256]{2,1,0:T(8,128)(2,1)S(1)} %get-tuple-element.23.full, bf16[2,2,8,40,256]{4,3,2,1,0:T(8,128)(2,1)S(1)} %get-tuple-element.24.whole, bf16[512,512]{1,0:T(8,128)(2,1)S(1)} %copy-done.1), custom_call_target="tpu_custom_call" | custom-call | tf_op jit(solution)/shard_map/pallas_call | solution.py:424
  (3 shorter events, 0.0 us)
Async XLA Ops:
  0.6 34.7 %copy-start.4 = (bf16[128,512]{1,0:T(8,128)(2,1)S(1)}, bf16[128,512]{1,0:T(8,128)(2,1)}, u32[]{:S(2)}) copy-start(bf16[128,512]{1,0:T(8,128)(2,1)} %w1.1) | copy-start | bytes 393220
  2.6 1.0 %copy-start.2 = (bf16[4,4,128,128]{3,2,1,0:T(8,128)(2,1)S(1)}, bf16[4,4,128,128]{3,2,1,0:T(8,128)(2,1)}, u32[]{:S(2)}) copy-start(bf16[4,4,128,128]{3,2,1,0:T(8,128)(2,1)} %tiles.1) | copy-start | bytes 1572868
  3.6 0.9 %copy-start.3 = (bf16[256,512]{1,0:T(8,128)(2,1)S(1)}, bf16[256,512]{1,0:T(8,128)(2,1)}, u32[]{:S(2)}) copy-start(bf16[256,512]{1,0:T(8,128)(2,1)} %cot.1) | copy-start | bytes 786436
  4.6 0.9 %copy-start.5 = (bf16[512,128]{1,0:T(8,128)(2,1)S(1)}, bf16[512,128]{1,0:T(8,128)(2,1)}, u32[]{:S(2)}) copy-start(bf16[512,128]{1,0:T(8,128)(2,1)} %feats.1) | copy-start | bytes 393220
  30.5 1.0 %copy-start = (bf16[512,512]{1,0:T(8,128)(2,1)S(1)}, bf16[512,512]{1,0:T(8,128)(2,1)}, u32[]{:S(2)}) copy-start(bf16[512,512]{1,0:T(8,128)(2,1)} %w2.3) | copy-start | bytes 1572868
  35.4 42.1 %copy-start.1 = (bf16[512,512]{1,0:T(8,128)(2,1)S(1)}, bf16[512,512]{1,0:T(8,128)(2,1)}, u32[]{:S(2)}) copy-start(bf16[512,512]{1,0:T(8,128)(2,1)} %w2.3) | copy-start | bytes 1572868

commit v4 on v3

--- a/solution.py
+++ b/solution.py
@@ -79,6 +79,7 @@
     greet([at(2), at(-2), at(far), at(flip)] + others)
     copies, n = [], 0
     pieces = ((tiles, all_tiles), (cols, all_cols), (cot, cots))
+    pieces = pieces if cot is not None else pieces[:2]
     for peer in others:
         for src, dst in pieces:
             copies.append(remote(src, dst.at[rep], send, recv, n, peer))
@@ -94,9 +95,28 @@
         copy.wait()
 
 
-def front_kernel(rows, reps, blocks, tile, tiles, cols, row_ids, band_ids, band, cots, w2,
-                 dense, first_o, terms_o, own_o, deg_o):
-    row, rep = lax.axis_index("row"), lax.axis_index("rep")
+def scale_terms(rep, reps, cots, w2, dense, degree, terms):
+    size = degree.shape[0]
+    half = w2.shape[0] // reps
+    at = pl.ds(pl.multiple_of(rep * half, half), half)
+    pulled = dot(cots[...].reshape(size, -1), w2[at, :], (1, 1))
+    scaled = (pulled / degree).astype(BF16)
+    scaled_t = scaled.astype(F32).T.astype(BF16)
+    for s in range(SPAN):
+        part = dot(scaled_t, dense[:, s * size:(s + 1) * size], (1, 0))
+        if s == HOPS:
+            own = part.T + scaled.astype(F32)
+        terms[s] = part.astype(BF16)
+    return own
+
+
+def share_kernel(rows, reps, feats, tiles, cols, band, all_tiles, all_cols, send, recv, local):
+    open_kernel(rows, reps, feats, None, tiles, cols, band, None, all_tiles, all_cols, send, recv, local)
+
+
+def front_kernel(rows, reps, blocks, tile, tiles, cols, row_ids, band_ids, band,
+                 dense, first_o, deg_o):
+    row = lax.axis_index("row")
     total = rows * blocks
     per = tiles.shape[2]
     dense[...] = jnp.zeros_like(dense)
@@ -118,16 +138,12 @@
     summed = dot(dense[...], flat, (1, 0))
     first = ((summed + band[HOPS].astype(F32)) / degree).astype(BF16)
     first_o[...] = first
-    half = w2.shape[0] // reps
-    at = pl.ds(pl.multiple_of(rep * half, half), half)
-    pulled = dot(cots[...].reshape(local, -1), w2[at, :], (1, 1))
-    scaled = (pulled / degree).astype(BF16)
-    scaled_t = scaled.astype(F32).T.astype(BF16)
-    for s in range(SPAN):
-        part = dot(scaled_t, dense[:, s * local:(s + 1) * local], (1, 0))
-        if s == HOPS:
-            own_o[...] = part.T + scaled.astype(F32)
-        terms_o[s] = part.astype(BF16)
+
+
+def full_front_kernel(rows, reps, blocks, tile, tiles, cols, row_ids, band_ids, band, cots, w2,
+                      dense, first_o, terms_o, own_o, deg_o):
+    front_kernel(rows, reps, blocks, tile, tiles, cols, row_ids, band_ids, band, dense, first_o, deg_o)
+    own_o[...] = scale_terms(lax.axis_index("rep"), reps, cots, w2, dense, deg_o[...], terms_o)
 
 
 def band_kernel(rows, first, terms, first_band, term_band, pair, joint, send, recv, local):
@@ -194,8 +210,8 @@
         copy.wait()
 
 
-def rest_kernel(rows, reps, first, terms, dense, w1, own, deg, cots, full, whole,
-                first_band, term_band, pair, joint, second_s, go, gi, go_pair, gi_pair, go_mine, gi_mine,
+def rest_kernel(rows, reps, first, dense, w1, w2, deg, cot, full, whole,
+                cots, terms, first_band, term_band, pair, joint, second_s, go, gi, go_pair, gi_pair, go_mine, gi_mine,
                 go_parts, gi_parts, send, recv, local):
     row, rep = lax.axis_index("row"), lax.axis_index("rep")
     flip, far, at = places(rows)
@@ -206,15 +222,22 @@
     peers = [(q * 2 + core, rep) for q in turns]
     others = [(row, lax.rem(rep + t, reps)) for t in range(1, reps)]
     greet([sibling, at(far)] + peers + others)
+    swaps = [remote(cot, cots.at[rep], send, recv, 12 + n, peer) for n, peer in enumerate(others)]
+    swaps.append(pltpu.make_async_copy(cot, cots.at[rep], local.at[2]))
+    for copy in swaps:
+        copy.start()
+    moved = start_rows(rows, first, first_band, send, recv, 3)
+    keep = pltpu.make_async_copy(first, first_band.at[HOPS], local.at[0])
+    keep.start()
+    for copy in swaps:
+        copy.wait()
+    own = scale_terms(rep, reps, cots, w2, dense, deg[...], terms)
     joined = [remote(terms.at[HOPS + shift + flip], pair.at[n], send, recv, n, sibling)
               for n, shift in enumerate((2, -2))]
     for copy in joined:
         copy.start()
-    moved = start_rows(rows, first, first_band, send, recv, 3)
     direct = [remote(terms.at[HOPS + far], term_band.at[2], send, recv, 2, at(far))]
     direct[0].start()
-    keep = pltpu.make_async_copy(first, first_band.at[HOPS], local.at[0])
-    keep.start()
     direct.append(remote(terms.at[HOPS + flip], term_band.at[3], send, recv, 7, sibling))
     direct[1].start()
     for n, shift in enumerate((2, -2)):
@@ -237,7 +260,7 @@
         summed = summed + dot(dense[:, s * size:(s + 1) * size], hidden, (1, 0))
     second = (summed / deg[...]).astype(BF16)
     second_s[...] = second.reshape(second_s.shape)
-    base = 12
+    base = 11 + reps
     late = [remote(second_s.at[peer[1]], full.at[rep], send, recv, base + n, peer) for n, peer in enumerate(others)]
     late.append(pltpu.make_async_copy(second_s.at[rep], full.at[rep], local.at[1]))
     for copy in late:
@@ -277,7 +300,7 @@
     got = term_band[0].astype(F32)
     for i in range(1, 4):
         got = got + term_band[i].astype(F32)
-    back = got.T + own[...]
+    back = got.T + own
     delta = jnp.where(preact > 0.0, back, 0.0).astype(BF16)
     gi[...] = dot(mine_first, delta, (0, 0)).reshape(gi.shape)
     rest = fold(gi, gi_pair, gi_mine, gi_parts, base)
@@ -363,6 +386,72 @@
     row_ids = ids[HOPS * local:(HOPS + 1) * local].reshape(local, 1)
     band_ids = ids.reshape(SPAN * blocks, tile)
     padded = jnp.pad(block_columns, ((0, 8 - blocks), (0, 128 - per)))
+    tall = hid * hid // reps // half + fin
+    if 6 < rows <= 16 and rows % 2 == 0 and fin % (8 * rows) == 0:
+        chips, deep, thin = rows // 2, hid // rows, fin // rows
+
+        band, all_tiles, all_cols = pl.pallas_call(
+            functools.partial(share_kernel, rows, reps),
+            out_shape=(
+                shape((SPAN, local, fin), BF16),
+                shape((reps,) + adjacency_tiles.shape, BF16),
+                shape((reps, 8, 128), jnp.int32),
+            ),
+            in_specs=[HBM] * 3,
+            out_specs=(VMEM,) * 2 + (ANY,),
+            scratch_shapes=sems(2 * (reps - 1) + 6),
+            compiler_params=params(0),
+        )(features, adjacency_tiles, padded)
+        dense, first, degree = pl.pallas_call(
+            functools.partial(front_kernel, rows, reps, blocks, tile),
+            out_shape=(
+                shape((local, SPAN * local), BF16),
+                shape((local, fin), BF16),
+                shape((local, 1), F32),
+            ),
+            in_specs=[VMEM, SMEM] + [VMEM] * 3,
+            out_specs=(VMEM,) * 3,
+            compiler_params=params(),
+        )(all_tiles, all_cols, row_ids, band_ids, band)
+
+        def bank(*dims):
+            return pltpu.VMEM(dims, F32)
+
+        full, whole = pl.pallas_call(
+            functools.partial(rest_kernel, rows, reps),
+            out_shape=(
+                shape((reps, quarter, half), BF16),
+                shape((reps, 2, chips, deep + thin, half), BF16),
+            ),
+            in_specs=[VMEM] * 6,
+            out_specs=(VMEM,) * 2,
+            scratch_shapes=[
+                pltpu.VMEM((reps, quarter, hid), BF16),
+                pltpu.VMEM((SPAN, half, local), BF16),
+                pltpu.VMEM((SPAN, local, fin), BF16),
+                pltpu.VMEM((4, half, local), BF16),
+                pltpu.VMEM((2, half, local), BF16),
+                pltpu.VMEM((2, half, local), BF16),
+                pltpu.VMEM((reps, quarter, half), BF16),
+                bank(2, chips, deep, half),
+                bank(2, chips, thin, half),
+                bank(chips, deep, half),
+                bank(chips, thin, half),
+                bank(chips, deep, half),
+                bank(chips, thin, half),
+                bank(chips - 1, deep, half),
+                bank(chips - 1, thin, half),
+            ] + sems(12 + 4 * reps + 3 * chips),
+            compiler_params=params(1),
+        )(first, dense, input_weight, output_weight, degree, cotangent)
+        scores, grad_input, grad_output = pl.pallas_call(
+            functools.partial(close_kernel, deep),
+            out_shape=(shape((quarter, hid), BF16), shape((fin, hid), F32), shape((hid, hid), F32)),
+            in_specs=[VMEM] * 3,
+            out_specs=(VMEM,) * 3,
+            compiler_params=params(),
+        )(full, whole, output_weight)
+        return scores, grad_input, grad_output
     band, cots, all_tiles, all_cols = pl.pallas_call(
         functools.partial(open_kernel, rows, reps),
         out_shape=(
@@ -377,7 +466,7 @@
         compiler_params=params(0),
     )(features, cotangent, adjacency_tiles, padded)
     dense, first, terms, own, degree = pl.pallas_call(
-        functools.partial(front_kernel, rows, reps, blocks, tile),
+        functools.partial(full_front_kernel, rows, reps, blocks, tile),
         out_shape=(
             shape((local, SPAN * local), BF16),
             shape((local, fin), BF16),
@@ -389,46 +478,6 @@
         out_specs=(VMEM,) * 5,
         compiler_params=params(),
     )(all_tiles, all_cols, row_ids, band_ids, band, cots, output_weight)
-    tall = hid * hid // reps // half + fin
-    if 6 < rows <= 16 and rows % 2 == 0 and fin % (8 * rows) == 0:
-        chips, deep, thin = rows // 2, hid // rows, fin // rows
-
-        def bank(*dims):
-            return pltpu.VMEM(dims, F32)
-
-        full, whole = pl.pallas_call(
-            functools.partial(rest_kernel, rows, reps),
-            out_shape=(
-                shape((reps, quarter, half), BF16),
-                shape((reps, 2, chips, deep + thin, half), BF16),
-            ),
-            in_specs=[VMEM] * 7,
-            out_specs=(VMEM,) * 2,
-            scratch_shapes=[
-                pltpu.VMEM((SPAN, local, fin), BF16),
-                pltpu.VMEM((4, half, local), BF16),
-                pltpu.VMEM((2, half, local), BF16),
-                pltpu.VMEM((2, half, local), BF16),
-                pltpu.VMEM((reps, quarter, half), BF16),
-                bank(2, chips, deep, half),
-                bank(2, chips, thin, half),
-                bank(chips, deep, half),
-                bank(chips, thin, half),
-                bank(chips, deep, half),
-                bank(chips, thin, half),
-                bank(chips - 1, deep, half),
-                bank(chips - 1, thin, half),
-            ] + sems(12 + 3 * reps + 3 * chips),
-            compiler_params=params(1),
-        )(first, terms, dense, input_weight, own, degree, cots)
-        scores, grad_input, grad_output = pl.pallas_call(
-            functools.partial(close_kernel, deep),
-            out_shape=(shape((quarter, hid), BF16), shape((fin, hid), F32), shape((hid, hid), F32)),
-            in_specs=[VMEM] * 3,
-            out_specs=(VMEM,) * 3,
-            compiler_params=params(),
-        )(full, whole, output_weight)
-        return scores, grad_input, grad_output
     first_band, term_band = pl.pallas_call(
         functools.partial(band_kernel, rows),
         out_shape=(shape((SPAN, local, fin), BF16), shape((4, half, local), BF16)),

time: 79.1 us -> 77.3 us (0.977)
  Pallas kernels: 72.3 us -> 67.5 us
  local copies, waits for them, and re-layouts: 5.54 us -> 8.44 us
    pallas_call x1, Pallas kernels: 25 us -> 19.4 us  [body(): pl.pallas_call(functools.partial(share_kernel, rows, reps), out_shape=(sh...]
    unnamed x12, local copies, waits for them, and re-layouts: 3.94 us -> 6.88 us
    pallas_call x1, Pallas kernels: 42 us -> 43.7 us  [body(): pl.pallas_call(functools.partial(rest_kernel, rows, reps), out_shape=(sha...]
where the time goes in v4:
time: 77.3 us; the launch traced here: 76.9 us
  Pallas kernels  67.5 us (87%)
  local copies, waits for them, and re-layouts  8.44 us (11%)
    pallas_call x1, Pallas kernels, body(): pl.pallas_call(functools.partial(rest_kernel, rows, reps), out_shape=(sha...  43.7 us
    pallas_call x1, Pallas kernels, body(): pl.pallas_call(functools.partial(share_kernel, rows, reps), out_shape=(sh...  19.4 us
    unnamed x12, local copies, waits for them, and re-layouts  6.88 us
    pallas_call x1, Pallas kernels, body(): pl.pallas_call(functools.partial(front_kernel, rows, reps, blocks, tile),...  3.07 us

profile of v4, /device:TPU:0, one launch (start us, length us, event | category | flops | bytes accessed | tf_op | source)
XLA Modules:
  0.0 76.9 jit_solution(15937561656123350207)
XLA Ops:
  0.6 0.7 pad.4.cols
  1.3 0.7 copy.13
  2.1 0.1 reduce
  2.2 0.1 convert_reduce_fusion
  2.4 0.1 copy.14.row_ids
  2.5 0.0 copy-start.2
  2.5 1.0 %copy-done.2 = bf16[4,4,128,128]{3,2,1,0:T(8,128)(2,1)S(1)} copy-done((bf16[4,4,128,128]{3,2,1,0:T(8,128)(2,1)S(1)}, bf16[4,4,128,128]{3,2,1,0:T(8,128)(2,1)}, u32[]{:S(2)}) %copy-start.2) | copy-done | bytes 524312
  3.6 0.0 copy-start.4
  3.6 0.9 %copy-done.4 = bf16[512,128]{1,0:T(8,128)(2,1)S(1)} copy-done((bf16[512,128]{1,0:T(8,128)(2,1)S(1)}, bf16[512,128]{1,0:T(8,128)(2,1)}, u32[]{:S(2)}) %copy-start.4) | copy-done | bytes 131096
  4.5 19.4 %shard_map.94 = (bf16[7,512,128]{2,1,0:T(8,128)(2,1)S(1)}, bf16[2,4,4,128,128]{4,3,2,1,0:T(8,128)(2,1)S(1)}, s32[2,8,128]{2,1,0:T(8,128)S(1)}) custom-call(bf16[512,128]{1,0:T(8,128)(2,1)S(1)} %copy-done.4, bf16[4,4,128,128]{3,2,1,0:T(8,128)(2,1)S(1)} %copy-done.2, s32[8,128]{1,0:T(8,128)S(1)} %pad.4.cols), custom_call_target="tpu_custom_call" | custom-call | tf_op jit(solution)/shard_map/pallas_call | solution.py:393
  23.9 3.1 %shard_map.95 = (bf16[512,3584]{1,0:T(8,128)(2,1)}, bf16[512,128]{1,0:T(8,128)(2,1)S(1)}, f32[512,1]{1,0:T(8,128)S(1)}) custom-call(bf16[2,4,4,128,128]{4,3,2,1,0:T(8,128)(2,1)S(1)} %get-tuple-element.11.tiles, s32[2,8,128]{2,1,0:T(8,128)S(1)} %get-tuple-element.12.cols, s32[512,1]{1,0:T(8,128)S(1)} %copy.14.row_ids, s32[28,128]{1,0:T(8,128)S(1)} %bitcast.3, ...), custom_call_target="tpu_custom_call" | custom-call | tf_op jit(solution)/shard_map/pallas_call | solution.py:405
  26.9 0.0 copy-start
  27.0 2.0 %copy-done = bf16[512,3584]{1,0:T(8,128)(2,1)S(1)} copy-done((bf16[512,3584]{1,0:T(8,128)(2,1)S(1)}, bf16[512,3584]{1,0:T(8,128)(2,1)}, u32[]{:S(2)}) %copy-start) | copy-done | bytes 3670040
  29.0 0.0 copy-start.1
  29.0 1.0 %copy-done.1 = bf16[512,512]{1,0:T(8,128)(2,1)S(1)} copy-done((bf16[512,512]{1,0:T(8,128)(2,1)S(1)}, bf16[512,512]{1,0:T(8,128)(2,1)}, u32[]{:S(2)}) %copy-start.1) | copy-done | bytes 524312
  30.0 0.0 copy-start.3
  30.0 0.9 %copy-done.3 = bf16[256,512]{1,0:T(8,128)(2,1)S(1)} copy-done((bf16[256,512]{1,0:T(8,128)(2,1)S(1)}, bf16[256,512]{1,0:T(8,128)(2,1)}, u32[]{:S(2)}) %copy-start.3) | copy-done | bytes 262168
  31.0 0.0 copy-start.5
  31.0 0.9 %copy-done.5 = bf16[128,512]{1,0:T(8,128)(2,1)S(1)} copy-done((bf16[128,512]{1,0:T(8,128)(2,1)S(1)}, bf16[128,512]{1,0:T(8,128)(2,1)}, u32[]{:S(2)}) %copy-start.5) | copy-done | bytes 131096
  31.9 43.7 %shard_map.96 = (bf16[2,256,256]{2,1,0:T(8,128)(2,1)S(1)}, bf16[2,2,8,40,256]{4,3,2,1,0:T(8,128)(2,1)S(1)}) custom-call(bf16[512,128]{1,0:T(8,128)(2,1)S(1)} %get-tuple-element.14.first, bf16[512,3584]{1,0:T(8,128)(2,1)S(1)} %copy-done, bf16[128,512]{1,0:T(8,128)(2,1)S(1)} %copy-done.5, bf16[512,512]{1,0:T(8,128)(2,1)S(1)} %copy-done.1, ...), custom_call_target="tpu_custom_call" | custom-call | tf_op jit(solution)/shard_map/pallas_call | solution.py:420
  75.5 1.4 %shard_map.97 = (bf16[256,512]{1,0:T(8,128)(2,1)}, f32[128,512]{1,0:T(8,128)}, f32[512,512]{1,0:T(8,128)}) custom-call(bf16[2,256,256]{2,1,0:T(8,128)(2,1)S(1)} %get-tuple-element.17.full, bf16[2,2,8,40,256]{4,3,2,1,0:T(8,128)(2,1)S(1)} %get-tuple-element.18.whole, bf16[512,512]{1,0:T(8,128)(2,1)S(1)} %copy-done.1), custom_call_target="tpu_custom_call" | custom-call | tf_op jit(solution)/shard_map/pallas_call | solution.py:447
  (3 shorter events, 0.0 us)
Async XLA Ops:
  2.5 1.0 %copy-start.2 = (bf16[4,4,128,128]{3,2,1,0:T(8,128)(2,1)S(1)}, bf16[4,4,128,128]{3,2,1,0:T(8,128)(2,1)}, u32[]{:S(2)}) copy-start(bf16[4,4,128,128]{3,2,1,0:T(8,128)(2,1)} %tiles.1) | copy-start | bytes 1572868
  3.6 0.9 %copy-start.4 = (bf16[512,128]{1,0:T(8,128)(2,1)S(1)}, bf16[512,128]{1,0:T(8,128)(2,1)}, u32[]{:S(2)}) copy-start(bf16[512,128]{1,0:T(8,128)(2,1)} %feats.1) | copy-start | bytes 393220
  26.9 2.0 %copy-start = (bf16[512,3584]{1,0:T(8,128)(2,1)S(1)}, bf16[512,3584]{1,0:T(8,128)(2,1)}, u32[]{:S(2)}) copy-start(bf16[512,3584]{1,0:T(8,128)(2,1)} %get-tuple-element.15.dense) | copy-start | bytes 11010052
  29.0 1.0 %copy-start.1 = (bf16[512,512]{1,0:T(8,128)(2,1)S(1)}, bf16[512,512]{1,0:T(8,128)(2,1)}, u32[]{:S(2)}) copy-start(bf16[512,512]{1,0:T(8,128)(2,1)} %w2.3) | copy-start | bytes 1572868
  30.0 0.9 %copy-start.3 = (bf16[256,512]{1,0:T(8,128)(2,1)S(1)}, bf16[256,512]{1,0:T(8,128)(2,1)}, u32[]{:S(2)}) copy-start(bf16[256,512]{1,0:T(8,128)(2,1)} %cot.1) | copy-start | bytes 786436
  31.0 0.9 %copy-start.5 = (bf16[128,512]{1,0:T(8,128)(2,1)S(1)}, bf16[128,512]{1,0:T(8,128)(2,1)}, u32[]{:S(2)}) copy-start(bf16[128,512]{1,0:T(8,128)(2,1)} %w1.1) | copy-start | bytes 393220

commit v5 on v4

--- a/solution.py
+++ b/solution.py
@@ -350,8 +350,7 @@
     scores_o[...] = total.astype(BF16)
 
 
-def params(number=None):
-    limit = 48 << 20
+def params(number=None, limit=48 << 20):
     if number is None:
         return pltpu.CompilerParams(vmem_limit_bytes=limit)
     return pltpu.CompilerParams(vmem_limit_bytes=limit, collective_id=number, has_side_effects=True)
@@ -442,7 +441,7 @@
                 bank(chips - 1, deep, half),
                 bank(chips - 1, thin, half),
             ] + sems(12 + 4 * reps + 3 * chips),
-            compiler_params=params(1),
+            compiler_params=params(1, 60 << 20),
         )(first, dense, input_weight, output_weight, degree, cotangent)
         scores, grad_input, grad_output = pl.pallas_call(
             functools.partial(close_kernel, deep),

time: 77.3 us -> 79 us (1.022)
  Pallas kernels: 67.5 us -> 70.8 us
  local copies, waits for them, and re-layouts: 8.44 us -> 6.9 us
    pallas_call x1, Pallas kernels: 43.7 us -> 47 us  [body(): pl.pallas_call(functools.partial(rest_kernel, rows, reps), out_shape=(sha...]
    unnamed x12 -> x14, local copies, waits for them, and re-layouts: 6.88 us -> 5.34 us
where the time goes in v5:
time: 79 us; the launch traced here: 78.7 us
  Pallas kernels  70.8 us (90%)
  local copies, waits for them, and re-layouts  6.9 us (9%)
    pallas_call x1, Pallas kernels, body(): pl.pallas_call(functools.partial(rest_kernel, rows, reps), out_shape=(sha...  47 us
    pallas_call x1, Pallas kernels, body(): pl.pallas_call(functools.partial(share_kernel, rows, reps), out_shape=(sh...  19.4 us
    unnamed x14, local copies, waits for them, and re-layouts  5.34 us
    pallas_call x1, Pallas kernels, body(): pl.pallas_call(functools.partial(front_kernel, rows, reps, blocks, tile),...  3.07 us

profile of v5, /device:TPU:0, one launch (start us, length us, event | category | flops | bytes accessed | tf_op | source)
XLA Modules:
  0.0 78.7 jit_solution(2017712771859845319)
XLA Ops:
  0.6 0.7 pad.4.cols
  1.3 0.7 copy.13
  2.1 0.1 reduce
  2.2 0.1 convert_reduce_fusion
  2.4 0.1 copy.14.row_ids
  2.5 0.0 copy-start.2
  2.5 1.0 %copy-done.2 = bf16[4,4,128,128]{3,2,1,0:T(8,128)(2,1)S(1)} copy-done((bf16[4,4,128,128]{3,2,1,0:T(8,128)(2,1)S(1)}, bf16[4,4,128,128]{3,2,1,0:T(8,128)(2,1)}, u32[]{:S(2)}) %copy-start.2) | copy-done | bytes 524312
  3.6 0.0 copy-start.5
  3.6 0.9 %copy-done.5 = bf16[512,128]{1,0:T(8,128)(2,1)S(1)} copy-done((bf16[512,128]{1,0:T(8,128)(2,1)S(1)}, bf16[512,128]{1,0:T(8,128)(2,1)}, u32[]{:S(2)}) %copy-start.5) | copy-done | bytes 131096
  4.5 19.4 %shard_map.94 = (bf16[7,512,128]{2,1,0:T(8,128)(2,1)S(1)}, bf16[2,4,4,128,128]{4,3,2,1,0:T(8,128)(2,1)S(1)}, s32[2,8,128]{2,1,0:T(8,128)S(1)}) custom-call(bf16[512,128]{1,0:T(8,128)(2,1)S(1)} %copy-done.5, bf16[4,4,128,128]{3,2,1,0:T(8,128)(2,1)S(1)} %copy-done.2, s32[8,128]{1,0:T(8,128)S(1)} %pad.4.cols), custom_call_target="tpu_custom_call" | custom-call | tf_op jit(solution)/shard_map/pallas_call | solution.py:392
  23.9 0.0 copy-start
  23.9 3.1 %shard_map.95 = (bf16[512,3584]{1,0:T(8,128)(2,1)}, bf16[512,128]{1,0:T(8,128)(2,1)S(1)}, f32[512,1]{1,0:T(8,128)S(1)}) custom-call(bf16[2,4,4,128,128]{4,3,2,1,0:T(8,128)(2,1)S(1)} %get-tuple-element.11.tiles, s32[2,8,128]{2,1,0:T(8,128)S(1)} %get-tuple-element.12.cols, s32[512,1]{1,0:T(8,128)S(1)} %copy.14.row_ids, s32[28,128]{1,0:T(8,128)S(1)} %bitcast.3, ...), custom_call_target="tpu_custom_call" | custom-call | tf_op jit(solution)/shard_map/pallas_call | solution.py:404
  27.0 0.0 copy-start.3
  27.0 0.7 copy-done.3
  27.7 0.0 copy-start.6
  27.7 0.7 copy-done.6
  28.3 47.0 %shard_map.96 = (bf16[2,256,256]{2,1,0:T(8,128)(2,1)}, bf16[2,2,8,40,256]{4,3,2,1,0:T(8,128)(2,1)}) custom-call(bf16[512,128]{1,0:T(8,128)(2,1)} %copy-done.6, bf16[512,3584]{1,0:T(8,128)(2,1)} %get-tuple-element.15.dense, bf16[128,512]{1,0:T(8,128)(2,1)} %w1.1, bf16[512,512]{1,0:T(8,128)(2,1)} %w2.3, f32[512,1]{1,0:T(8,128)} %copy-done.3, bf16[256,512]{1,0:T(8,128)(2,1)} %cot.1), custom_call_target="tpu_custom_call" | custom-call | tf_op jit(solution)/shard_map/pallas_call | solution.py:419
  75.3 0.0 copy-done
  75.3 0.0 copy-start.1
  75.3 1.1 %copy-done.1 = bf16[2,2,8,40,256]{4,3,2,1,0:T(8,128)(2,1)S(1)} copy-done((bf16[2,2,8,40,256]{4,3,2,1,0:T(8,128)(2,1)S(1)}, bf16[2,2,8,40,256]{4,3,2,1,0:T(8,128)(2,1)}, u32[]{:S(2)}) %copy-start.1) | copy-done | bytes 655384
  76.4 0.0 copy-start.4
  76.4 0.9 %copy-done.4 = bf16[2,256,256]{2,1,0:T(8,128)(2,1)S(1)} copy-done((bf16[2,256,256]{2,1,0:T(8,128)(2,1)S(1)}, bf16[2,256,256]{2,1,0:T(8,128)(2,1)}, u32[]{:S(2)}) %copy-start.4) | copy-done | bytes 262168
  77.3 1.4 %shard_map.97 = (bf16[256,512]{1,0:T(8,128)(2,1)}, f32[128,512]{1,0:T(8,128)}, f32[512,512]{1,0:T(8,128)}) custom-call(bf16[2,256,256]{2,1,0:T(8,128)(2,1)S(1)} %copy-done.4, bf16[2,2,8,40,256]{4,3,2,1,0:T(8,128)(2,1)S(1)} %copy-done.1, bf16[512,512]{1,0:T(8,128)(2,1)S(1)} %copy-done), custom_call_target="tpu_custom_call" | custom-call | tf_op jit(solution)/shard_map/pallas_call | solution.py:446
  (3 shorter events, 0.0 us)
Async XLA Ops:
  2.5 1.0 %copy-start.2 = (bf16[4,4,128,128]{3,2,1,0:T(8,128)(2,1)S(1)}, bf16[4,4,128,128]{3,2,1,0:T(8,128)(2,1)}, u32[]{:S(2)}) copy-start(bf16[4,4,128,128]{3,2,1,0:T(8,128)(2,1)} %tiles.1) | copy-start | bytes 1572868
  3.6 0.9 %copy-start.5 = (bf16[512,128]{1,0:T(8,128)(2,1)S(1)}, bf16[512,128]{1,0:T(8,128)(2,1)}, u32[]{:S(2)}) copy-start(bf16[512,128]{1,0:T(8,128)(2,1)} %feats.1) | copy-start | bytes 393220
  23.9 51.4 %copy-start = (bf16[512,512]{1,0:T(8,128)(2,1)S(1)}, bf16[512,512]{1,0:T(8,128)(2,1)}, u32[]{:S(2)}) copy-start(bf16[512,512]{1,0:T(8,128)(2,1)} %w2.3) | copy-start | bytes 1572868
  27.0 0.7 copy-start.3
  27.7 0.7 copy-start.6
  75.3 1.1 %copy-start.1 = (bf16[2,2,8,40,256]{4,3,2,1,0:T(8,128)(2,1)S(1)}, bf16[2,2,8,40,256]{4,3,2,1,0:T(8,128)(2,1)}, u32[]{:S(2)}) copy-start(bf16[2,2,8,40,256]{4,3,2,1,0:T(8,128)(2,1)} %get-tuple-element.18.whole) | copy-start | bytes 1966084
  76.4 0.9 %copy-start.4 = (bf16[2,256,256]{2,1,0:T(8,128)(2,1)S(1)}, bf16[2,256,256]{2,1,0:T(8,128)(2,1)}, u32[]{:S(2)}) copy-start(bf16[2,256,256]{2,1,0:T(8,128)(2,1)} %get-tuple-element.17.full) | copy-start | bytes 786436
